TPU v7x, 256 devices: a whole 4x4x8 slice. The times are simulated.
256 devices in a mesh: mic: 8 (over x, core), bin: 32 (over z, y).
Axes of the slice: x: 4, y: 4, z: 8, core: 2. Of those that a mesh axis runs over, the one named last changes fastest.
Arguments:
- images: bfloat16 [1024, 256, 256], P(('mic', 'bin')), may hold values from -6 to 6
- offsets: int32 [2, 1024], P(None, ('mic', 'bin')), may hold values from 0 to 255
- ctf_group: int32 [1024], P(('mic', 'bin')), may hold values from 0 to 63
- particle_bin: int32 [1024], P(('mic', 'bin')), may hold values from 0 to 2047, as said below
- bin_place: int32 [2048], replicated, may hold values from 0 to 2047, as said below
- defocus: float32 [64], replicated, may hold values from 40 to 160
- bfactor: float32 [64], replicated, may hold values from 0.2 to 2
- references: bfloat16 [2048, 256, 256], P(('mic', 'bin')), may hold values from -6 to 6
Outputs:
- refined: bfloat16 [2048, 256, 256], P(('mic', 'bin'))
- scores: float32 [1024], P(('mic', 'bin'))
Inputs may be any that keep to these rules, and one draw needn't show every extreme that they name: bin_place is a permutation. A particle's owner is bin_place[particle_bin] // 8, with bin index owner % 32 and mic index owner // 32. Of the 4 particles of one device, at most 1 have owners with one bin index, and some device of every mic row reaches it. `particle_bin`: within one mic row exactly 4 particles have owners with each bin index, and at most 1 have the same owner; in every mic row some owner has exactly 1. Several particles may share one bin.
All inputs are finite; a program needn't handle non-finite values.
Results may differ from a plain program's by a relative error of at most 0.0055.
Values may be sent and summed in bfloat16 or wider, within the bound.
A program may use at most 64 MiB of HBM per device.

v0:
```python
import math

import jax
import jax.numpy as jnp
from jax import lax
from jax.sharding import PartitionSpec as P

ITERS = 2


PRIOR_WEIGHT = 0.5
EPSILON = 1e-06
CONTRAST = 0.1
AMPLITUDE = math.sqrt(1.0 - CONTRAST * CONTRAST)


def hartley(image_side):
    row_index = lax.broadcasted_iota(jnp.int32, (image_side, image_side), 0)
    column_index = lax.broadcasted_iota(jnp.int32, (image_side, image_side), 1)
    phases = row_index * column_index % image_side
    angles = phases.astype(jnp.float32) * (2.0 * math.pi / image_side)
    return ((jnp.cos(angles) + jnp.sin(angles)) / math.sqrt(image_side)).astype(jnp.bfloat16)


def radius_square(image_side):
    frequency = jnp.arange(image_side, dtype=jnp.int32)
    folded = jnp.minimum(frequency, image_side - frequency).astype(jnp.float32)
    nyquist = image_side / 2.0
    square = (folded[:, None] * folded[:, None] + folded[None, :] * folded[None, :]) / (
        nyquist * nyquist
    )
    return square.reshape(image_side * image_side)


def ctf_rows(focus, damping, image_side):
    radial = radius_square(image_side)
    aberration = focus[:, None] * radial[None, :]
    envelope = jnp.exp(-damping[:, None] * radial[None, :])
    return -(AMPLITUDE * jnp.sin(aberration) + CONTRAST * jnp.cos(aberration)) * envelope


def group_lookup(groups, table):
    onehot = (groups[:, None] == jnp.arange(table.shape[0], dtype=jnp.int32)[None, :]).astype(
        jnp.float32
    )
    return jnp.sum(onehot * table[None, :], axis=1)


def group_ctf(groups, defocus, bfactor, image_side):
    return ctf_rows(group_lookup(groups, defocus), group_lookup(groups, bfactor), image_side)


def shifted(picture, shift_pair):
    image_side = picture.shape[0]
    doubled = jnp.concatenate([picture, picture], axis=0)
    rows_moved = lax.dynamic_slice_in_dim(doubled, shift_pair[0], image_side, 0)
    doubled = jnp.concatenate([rows_moved, rows_moved], axis=1)
    return lax.dynamic_slice_in_dim(doubled, shift_pair[1], image_side, 1)


def transform(images, offsets):
    basis = hartley(images.shape[1])
    moved = jax.vmap(shifted)(images, offsets.T)
    partial_rows = jnp.einsum(
        "kx,pxy->pky", basis, moved, preferred_element_type=jnp.float32
    ).astype(jnp.bfloat16)
    return jnp.einsum(
        "pky,ly->pkl", partial_rows, basis, preferred_element_type=jnp.float32
    ).astype(jnp.bfloat16)


def compare(ref_rows, ctf_table, spectra, image_side):
    predicted = ctf_table * ref_rows.astype(jnp.float32)
    values = spectra.astype(jnp.float32)
    cross_term = jnp.mean(predicted * values, axis=1)
    model_power = jnp.mean(predicted * predicted, axis=1) + EPSILON
    data_power = jnp.mean(values * values, axis=1) + EPSILON
    correlation = cross_term / jnp.sqrt(model_power * data_power)
    weights = jax.nn.sigmoid(image_side * correlation).astype(jnp.bfloat16)
    weighted = (weights.astype(jnp.float32)[:, None] * ctf_table * values).astype(jnp.bfloat16)
    return (correlation, weights, weighted)


def accumulate(current, local_bin, active, weights, weighted, ctf_table):
    own_bins = current.shape[0]
    member = (local_bin[None, :] == jnp.arange(own_bins, dtype=jnp.int32)[:, None]) & (
        active[None, :] > 0
    )
    numerator = jnp.dot(member.astype(jnp.bfloat16), weighted, preferred_element_type=jnp.float32)
    ctf_power = weights.astype(jnp.float32)[:, None] * ctf_table * ctf_table
    denominator = jnp.dot(member.astype(jnp.float32), ctf_power, precision=lax.Precision.HIGHEST)
    previous = current.reshape(own_bins, -1).astype(jnp.float32)
    updated = (numerator + PRIOR_WEIGHT * previous) / (denominator + PRIOR_WEIGHT)
    return updated.astype(jnp.bfloat16).reshape(current.shape)


def bucket(targets, active, buckets, capacity):
    matches = (targets[:, None] == jnp.arange(buckets, dtype=jnp.int32)[None, :]).astype(
        jnp.int32
    ) * active[:, None]
    before = jnp.cumsum(matches, axis=0) - matches
    ranking = jnp.sum(before * matches, axis=1)
    destination = targets * capacity + ranking
    slot_ids = jnp.arange(buckets * capacity, dtype=jnp.int32)
    return ((destination[None, :] == slot_ids[:, None]) & (active[None, :] > 0)).astype(jnp.int32)


def pick_ints(selector, values):
    return jnp.sum(selector[:, :, None] * values[None, :, :], axis=1)


def pick_rows(selector, values):
    return jnp.dot(
        selector.astype(jnp.bfloat16), values, preferred_element_type=jnp.float32
    ).astype(jnp.bfloat16)


def body(images, offsets, ctf_group, particle_bin, bin_place, defocus, bfactor, references):
    mic_count = lax.axis_size("mic")
    bin_count = lax.axis_size("bin")
    particles_here = images.shape[0]
    image_side = images.shape[1]
    pixel_count = image_side * image_side
    own_bins = references.shape[0]
    cap_first = (particles_here + bin_count - 1) // bin_count
    cap_second = (3 * particles_here + 2 * mic_count - 1) // (2 * mic_count)
    first_total = bin_count * cap_first
    second_total = mic_count * cap_second
    transformed = transform(images, offsets)
    flat_images = transformed.reshape(particles_here, pixel_count)
    places = jnp.take(bin_place, particle_bin)
    owners = places // own_bins
    target_bin = owners % bin_count
    target_mic = owners // bin_count
    local_bin = places % own_bins
    active = jnp.ones((particles_here,), jnp.int32)
    first_pick = bucket(target_bin, active, bin_count, cap_first)
    labels = jnp.stack([active, target_mic, local_bin, ctf_group], axis=1)
    first_labels = pick_ints(first_pick, labels).reshape(bin_count, cap_first, 4)
    row_labels = lax.all_to_all(
        first_labels, "bin", split_axis=0, concat_axis=0, tiled=True
    ).reshape(first_total, 4)
    second_pick = bucket(row_labels[:, 1], row_labels[:, 0], mic_count, cap_second)
    second_labels = pick_ints(second_pick, row_labels).reshape(mic_count, cap_second, 4)
    slot_labels = lax.all_to_all(
        second_labels, "mic", split_axis=0, concat_axis=0, tiled=True
    ).reshape(second_total, 4)
    slot_ctf = group_ctf(slot_labels[:, 3], defocus, bfactor, image_side)
    home_ctf = group_ctf(ctf_group, defocus, bfactor, image_side)
    current = references
    scores = jnp.zeros((particles_here,), jnp.float32)
    for iteration in range(ITERS):
        ref_rows = jnp.take(current.reshape(own_bins, pixel_count), slot_labels[:, 2], axis=0)
        toward_row = lax.all_to_all(
            ref_rows.reshape(mic_count, cap_second, pixel_count),
            "mic",
            split_axis=0,
            concat_axis=0,
            tiled=True,
        )
        row_refs = pick_rows(second_pick.T, toward_row.reshape(second_total, pixel_count))
        toward_home = lax.all_to_all(
            row_refs.reshape(bin_count, cap_first, pixel_count),
            "bin",
            split_axis=0,
            concat_axis=0,
            tiled=True,
        )
        home_refs = pick_rows(first_pick.T, toward_home.reshape(first_total, pixel_count))
        scores, weights, weighted = compare(home_refs, home_ctf, flat_images, image_side)
        sent_terms = pick_rows(first_pick, weighted).reshape(bin_count, cap_first, pixel_count)
        sent_weights = pick_rows(first_pick, weights[:, None])
        row_terms, row_weights = (
            lax.all_to_all(sent_terms, "bin", split_axis=0, concat_axis=0, tiled=True),
            lax.all_to_all(sent_weights, "bin", split_axis=0, concat_axis=0, tiled=True),
        )
        row_terms = row_terms.reshape(first_total, pixel_count)
        next_terms = pick_rows(second_pick, row_terms).reshape(mic_count, cap_second, pixel_count)
        next_weights = pick_rows(second_pick, row_weights)
        owner_terms, owner_weights = (
            lax.all_to_all(next_terms, "mic", split_axis=0, concat_axis=0, tiled=True),
            lax.all_to_all(next_weights, "mic", split_axis=0, concat_axis=0, tiled=True),
        )
        current = accumulate(
            current,
            slot_labels[:, 2],
            slot_labels[:, 0],
            owner_weights.reshape(second_total),
            owner_terms.reshape(second_total, pixel_count),
            slot_ctf,
        )
    return (current, scores)


def solution(mesh):
    in_specs = (
        P(("mic", "bin"), None, None),
        P(None, ("mic", "bin")),
        P(("mic", "bin")),
        P(("mic", "bin")),
        P(),
        P(),
        P(),
        P(("mic", "bin"), None, None),
    )
    out_specs = (P(("mic", "bin"), None, None), P(("mic", "bin")))
    return jax.shard_map(body, mesh=mesh, in_specs=in_specs, out_specs=out_specs, check_vma=False)
```

profile of v0, /device:TPU:1, one launch (start us, length us, event | category | flops | bytes accessed | tf_op | source)
XLA Modules:
  0.0 787.8 jit_solution(7092401442758363564)
XLA Ops:
  4.0 20.4 %all_to_all.86 = s32[32,1,4]{2,1,0:T(1,128)S(1)} all-to-all(s32[32,1,4]{2,1,0:T(1,128)S(1)} %copy.71), channel_id=1, replica_groups=mesh['mic'=8,'bin'=32] {'bin'}, dimensions={0} | all-to-all | bytes 1024 | tf_op jit(solution)/shard_map/all_to_all | solution.py:140
  41.1 18.9 %all_to_all.87 = bf16[8,2,32768]{2,1,0:T(2,128)(2,1)} all-to-all(bf16[8,2,32768]{2,1,0:T(2,128)(2,1)S(1)} %reshape.477), channel_id=1, replica_groups=mesh['mic'=8,'bin'=32] {'mic'}, dimensions={0} | all-to-all | bytes 2097152 | tf_op jit(solution)/shard_map/all_to_all | solution.py:154
  100.1 78.8 %all-to-all-done.3 = bf16[32,2,32768]{2,1,0:T(2,128)(2,1)} async-done(((bf16[32,2,32768]{2,1,0:T(2,128)(2,1)}), bf16[32,2,32768]{2,1,0:T(2,128)(2,1)}, u32[]{:S(2)}, u32[]{:S(2)}) %all-to-all-start.3) | async-done | bytes 4194336 | tf_op jit(solution)/shard_map/all_to_all | solution.py:162
  178.9 19.8 %reshape.480 = bf16[32,1,65536]{2,1,0:T(2,128)(2,1)} reshape(bf16[32,2,32768]{2,1,0:T(2,128)(2,1)} %all-to-all-done.3) | data formatting | bytes 8388608
  198.7 12.5 %multiply_reduce_fusion.3 = (f32[4]{0:T(128)S(1)}, f32[4]{0:T(128)S(1)}) fusion(f32[4,65536]{1,0:T(4,128)S(1)} %bitcast.146, bf16[32,1,65536]{2,1,0:T(2,128)(2,1)} %reshape.480, s32[4]{0:T(128)S(1)} %add.183, f32[4]{0:T(128)S(1)} %neg.41, f32[65536]{0:T(1024)S(1)} %bitcast.151, f32[4]{0:T(128)S(1)} %get-tuple-element.17), kind=kOutput, calls=%fused_computation.102 | convolution fusion | flops 20447608 | bytes 5505104 | tf_op jit(solution)/shard_map/dot_general | solution.py:113
  211.2 11.3 %fusion.1 = bf16[32,1,65536]{2,0,1:T(8,128)(2,1)} fusion(f32[4,65536]{1,0:T(4,128)S(1)} %bitcast.147, f32[4]{0:T(128)S(1)} %get-tuple-element.24, f32[4]{0:T(128)S(1)} %neg.41, f32[65536]{0:T(1024)S(1)} %bitcast.152, f32[4]{0:T(128)S(1)} %get-tuple-element.17, s32[4]{0:T(128)S(1)} %add.183), kind=kOutput, calls=%fused_computation.10 | convolution fusion | flops 21496192 | bytes 5505088 | tf_op jit(solution)/shard_map/dot_general | solution.py:113
  223.4 8.6 %all-to-all-start.6 = ((bf16[32,1,1]{2,1,0:T(2,128)(2,1)}), bf16[32,1,1]{2,1,0:T(2,128)(2,1)S(1)}, u32[]{:S(2)}, u32[]{:S(2)}) async-start(bf16[32,1,1]{2,1,0:T(2,128)(2,1)} %copy.84), calls=%async_computation.6 | async-start | bytes 32768 | tf_op jit(solution)/shard_map/all_to_all | solution.py:175
  232.0 6.8 reduce.9
  245.4 9.3 %all-to-all-start.4 = ((bf16[32,2,32768]{2,1,0:T(2,128)(2,1)}), bf16[32,2,32768]{2,1,0:T(2,128)(2,1)}, u32[]{:S(2)}, u32[]{:S(2)}) async-start(bf16[32,2,32768]{2,1,0:T(2,128)(2,1)} %reshape.481), calls=%async_computation.4 | async-start | bytes 8388608 | tf_op jit(solution)/shard_map/all_to_all | solution.py:174
  255.9 91.0 %all-to-all-done.4 = bf16[32,2,32768]{2,1,0:T(2,128)(2,1)} async-done(((bf16[32,2,32768]{2,1,0:T(2,128)(2,1)}), bf16[32,2,32768]{2,1,0:T(2,128)(2,1)}, u32[]{:S(2)}, u32[]{:S(2)}) %all-to-all-start.4) | async-done | bytes 4194336 | tf_op jit(solution)/shard_map/all_to_all | solution.py:174
  353.2 19.8 %reshape.482 = bf16[32,1,65536]{2,1,0:T(2,128)(2,1)} reshape(bf16[32,2,32768]{2,1,0:T(2,128)(2,1)} %all-to-all-done.4) | data formatting | bytes 8388608
  373.0 7.9 %fusion.8 = bf16[8,1,65536]{2,0,1:T(8,128)(2,1)S(1)} fusion(bf16[32,1,65536]{2,1,0:T(2,128)(2,1)} %reshape.482, pred[32]{0:T(512)(128)(4,1)S(1)} %broadcast_compare_fusion, s32[32]{0:T(128)S(1)} %fusion.157), kind=kOutput, calls=%fused_computation.23 | convolution fusion | flops 34079744 | bytes 5243040 | tf_op jit(solution)/shard_map/dot_general | solution.py:113
  389.6 11.4 %convolution_add_fusion.2 = f32[8,65536]{1,0:T(8,128)} fusion(f32[8]{0:T(128)S(1)} %neg.44, f32[65536]{0:T(1024)S(1)} %bitcast.153, f32[8]{0:T(128)S(1)} %get-tuple-element.19, f32[8]{0:T(128)S(1)} %convert_reduce_fusion.1, s32[8]{0:T(128)S(1)} %get-tuple-element.31, pred[8]{0:T(512)(128)(4,1)S(1)} %compare_bitcast_fusion), kind=kOutput, calls=%fused_computation.15 | convolution fusion | flops 55574656 | bytes 2359432 | tf_op jit(solution)/shard_map/dot_general | solution.py:91
  415.2 18.4 %all_to_all.88 = bf16[8,2,32768]{2,1,0:T(2,128)(2,1)S(1)} all-to-all(bf16[8,2,32768]{2,1,0:T(2,128)(2,1)S(1)} %reshape.485), channel_id=1, replica_groups=mesh['mic'=8,'bin'=32] {'mic'}, dimensions={0} | all-to-all | bytes 2097152 | tf_op jit(solution)/shard_map/all_to_all | solution.py:154
  455.5 99.9 %all_to_all.89 = bf16[32,2,32768]{2,1,0:T(2,128)(2,1)} all-to-all(bf16[32,2,32768]{2,1,0:T(2,128)(2,1)} %reshape.487), channel_id=1, replica_groups=mesh['mic'=8,'bin'=32] {'bin'}, dimensions={0} | all-to-all | bytes 8388608 | tf_op jit(solution)/shard_map/all_to_all | solution.py:162
  555.4 19.9 %reshape.488 = bf16[32,1,65536]{2,1,0:T(2,128)(2,1)} reshape(bf16[32,2,32768]{2,1,0:T(2,128)(2,1)} %all_to_all.89) | data formatting | bytes 8388608
  575.3 12.5 %multiply_reduce_fusion.1 = (f32[4]{0:T(128)S(1)}, f32[4]{0:T(128)S(1)}) fusion(f32[4,65536]{1,0:T(4,128)S(1)} %bitcast.148, bf16[32,1,65536]{2,1,0:T(2,128)(2,1)} %reshape.488, s32[4]{0:T(128)S(1)} %add.183, f32[4]{0:T(128)S(1)} %neg.41, f32[65536]{0:T(1024)S(1)} %bitcast.154, f32[4]{0:T(128)S(1)} %get-tuple-element.17), kind=kOutput, calls=%fused_computation.88 | convolution fusion | flops 20447608 | bytes 5505104 | tf_op jit(solution)/shard_map/dot_general | solution.py:113
  588.3 10.9 %fusion.3 = bf16[32,1,65536]{2,0,1:T(8,128)(2,1)} fusion(f32[4,65536]{1,0:T(4,128)S(1)} %bitcast.149, f32[4]{0:T(128)S(1)} %get-tuple-element.21, f32[4]{0:T(128)S(1)} %neg.41, f32[65536]{0:T(1024)S(1)} %bitcast.155, f32[4]{0:T(128)S(1)} %get-tuple-element.17, s32[4]{0:T(128)S(1)} %add.183), kind=kOutput, calls=%fused_computation.12 | convolution fusion | flops 21496192 | bytes 5505088 | tf_op jit(solution)/shard_map/dot_general | solution.py:113
  606.5 6.8 reduce.13
  619.9 9.3 %all-to-all-start.10 = ((bf16[32,2,32768]{2,1,0:T(2,128)(2,1)}), bf16[32,2,32768]{2,1,0:T(2,128)(2,1)}, u32[]{:S(2)}, u32[]{:S(2)}) async-start(bf16[32,2,32768]{2,1,0:T(2,128)(2,1)} %reshape.489), calls=%async_computation.10 | async-start | bytes 8388608 | tf_op jit(solution)/shard_map/all_to_all | solution.py:174
  630.4 91.2 %all-to-all-done.10 = bf16[32,2,32768]{2,1,0:T(2,128)(2,1)} async-done(((bf16[32,2,32768]{2,1,0:T(2,128)(2,1)}), bf16[32,2,32768]{2,1,0:T(2,128)(2,1)}, u32[]{:S(2)}, u32[]{:S(2)}) %all-to-all-start.10) | async-done | bytes 4194336 | tf_op jit(solution)/shard_map/all_to_all | solution.py:174
  728.1 19.8 %reshape.490 = bf16[32,1,65536]{2,1,0:T(2,128)(2,1)} reshape(bf16[32,2,32768]{2,1,0:T(2,128)(2,1)} %all-to-all-done.10) | data formatting | bytes 8388608
  747.8 7.9 %fusion.9 = bf16[8,1,65536]{2,0,1:T(8,128)(2,1)S(1)} fusion(bf16[32,1,65536]{2,1,0:T(2,128)(2,1)} %reshape.490, pred[32]{0:T(512)(128)(4,1)S(1)} %broadcast_compare_fusion, s32[32]{0:T(128)S(1)} %fusion.157), kind=kOutput, calls=%fused_computation.24 | convolution fusion | flops 34079744 | bytes 5243040 | tf_op jit(solution)/shard_map/dot_general | solution.py:113
  764.0 11.4 %convolution_add_fusion = f32[8,65536]{1,0:T(8,128)} fusion(f32[8]{0:T(128)S(1)} %convert_reduce_fusion, f32[8]{0:T(128)S(1)} %neg.44, f32[65536]{0:T(1024)S(1)} %bitcast.156, f32[8]{0:T(128)S(1)} %get-tuple-element.19, s32[8]{0:T(128)S(1)} %get-tuple-element.31, pred[8]{0:T(512)(128)(4,1)S(1)} %compare_bitcast_fusion), kind=kOutput, calls=%fused_computation.13 | convolution fusion | flops 55574656 | bytes 2359432 | tf_op jit(solution)/shard_map/dot_general | solution.py:91
  (122 shorter events, 162.0 us)
Async XLA Ops:
  0.6 0.7 copy-start
  25.7 10.9 %all-to-all-start.1 = ((s32[8,1,4]{2,1,0:T(1,128)}), s32[8,1,4]{2,1,0:T(1,128)S(1)}, u32[]{:S(2)}, u32[]{:S(2)}) async-start(s32[8,1,4]{2,1,0:T(1,128)} %copy.73), calls=%async_computation.1 | async-start | bytes 8192 | tf_op jit(solution)/shard_map/all_to_all | solution.py:145
  81.1 5.2 copy-start.4
  81.1 97.8 %all-to-all-start.3 = ((bf16[32,2,32768]{2,1,0:T(2,128)(2,1)}), bf16[32,2,32768]{2,1,0:T(2,128)(2,1)}, u32[]{:S(2)}, u32[]{:S(2)}) async-start(bf16[32,2,32768]{2,1,0:T(2,128)(2,1)} %reshape.479), calls=%async_computation.3 | async-start | bytes 8388608 | tf_op jit(solution)/shard_map/all_to_all | solution.py:162
  86.3 1.1 copy-start.8
  98.8 1.1 copy-start.5
  98.8 1.1 copy-start.6
  98.8 1.1 copy-start.7
  99.6 111.5 %copy-start.2 = (f32[1,4,256,256]{3,1,2,0:T(4,128)}, f32[1,4,256,256]{3,1,2,0:T(4,128)S(1)}, u32[]{:S(2)}) copy-start(f32[1,4,256,256]{3,1,2,0:T(4,128)S(1)} %copy.104) | copy-start | bytes 3145732
  223.4 22.0 %all-to-all-start.6 = ((bf16[32,1,1]{2,1,0:T(2,128)(2,1)}), bf16[32,1,1]{2,1,0:T(2,128)(2,1)S(1)}, u32[]{:S(2)}, u32[]{:S(2)}) async-start(bf16[32,1,1]{2,1,0:T(2,128)(2,1)} %copy.84), calls=%async_computation.6 | async-start | bytes 32768 | tf_op jit(solution)/shard_map/all_to_all | solution.py:175
  245.4 101.5 %all-to-all-start.4 = ((bf16[32,2,32768]{2,1,0:T(2,128)(2,1)}), bf16[32,2,32768]{2,1,0:T(2,128)(2,1)}, u32[]{:S(2)}, u32[]{:S(2)}) async-start(bf16[32,2,32768]{2,1,0:T(2,128)(2,1)} %reshape.481), calls=%async_computation.4 | async-start | bytes 8388608 | tf_op jit(solution)/shard_map/all_to_all | solution.py:174
  346.9 37.3 %all-to-all-start.7 = ((bf16[8,1,1]{2,1,0:T(2,128)(2,1)}), bf16[8,1,1]{2,1,0:T(2,128)(2,1)S(1)}, u32[]{:S(2)}, u32[]{:S(2)}) async-start(bf16[8,1,1]{2,1,0:T(2,128)(2,1)} %copy.85), calls=%async_computation.7 | async-start | bytes 8192 | tf_op jit(solution)/shard_map/all_to_all | solution.py:182
  384.3 20.1 %all-to-all-start.5 = ((bf16[8,2,32768]{2,1,0:T(2,128)(2,1)}), bf16[8,2,32768]{2,1,0:T(2,128)(2,1)S(1)}, u32[]{:S(2)}, u32[]{:S(2)}) async-start(bf16[8,2,32768]{2,1,0:T(2,128)(2,1)} %reshape.483), calls=%async_computation.5 | async-start | bytes 2097152 | tf_op jit(solution)/shard_map/all_to_all | solution.py:181
  555.4 19.9 %copy-start.3 = (f32[1,4,256,256]{3,1,2,0:T(4,128)S(1)}, f32[1,4,256,256]{3,1,2,0:T(4,128)}, u32[]{:S(2)}) copy-start(f32[1,4,256,256]{3,1,2,0:T(4,128)} %copy-done.2) | copy-start | bytes 3145732
  600.0 19.9 %all-to-all-start.12 = ((bf16[32,1,1]{2,1,0:T(2,128)(2,1)}), bf16[32,1,1]{2,1,0:T(2,128)(2,1)S(1)}, u32[]{:S(2)}, u32[]{:S(2)}) async-start(bf16[32,1,1]{2,1,0:T(2,128)(2,1)} %copy.90), calls=%async_computation.12 | async-start | bytes 32768 | tf_op jit(solution)/shard_map/all_to_all | solution.py:175
  619.9 101.7 %all-to-all-start.10 = ((bf16[32,2,32768]{2,1,0:T(2,128)(2,1)}), bf16[32,2,32768]{2,1,0:T(2,128)(2,1)}, u32[]{:S(2)}, u32[]{:S(2)}) async-start(bf16[32,2,32768]{2,1,0:T(2,128)(2,1)} %reshape.489), calls=%async_computation.10 | async-start | bytes 8388608 | tf_op jit(solution)/shard_map/all_to_all | solution.py:174
  721.6 37.5 %all-to-all-start.13 = ((bf16[8,1,1]{2,1,0:T(2,128)(2,1)}), bf16[8,1,1]{2,1,0:T(2,128)(2,1)S(1)}, u32[]{:S(2)}, u32[]{:S(2)}) async-start(bf16[8,1,1]{2,1,0:T(2,128)(2,1)} %copy.91), calls=%async_computation.13 | async-start | bytes 8192 | tf_op jit(solution)/shard_map/all_to_all | solution.py:182
  759.1 19.9 %all-to-all-start.11 = ((bf16[8,2,32768]{2,1,0:T(2,128)(2,1)}), bf16[8,2,32768]{2,1,0:T(2,128)(2,1)S(1)}, u32[]{:S(2)}, u32[]{:S(2)}) async-start(bf16[8,2,32768]{2,1,0:T(2,128)(2,1)} %reshape.491), calls=%async_computation.11 | async-start | bytes 2097152 | tf_op jit(solution)/shard_map/all_to_all | solution.py:181
  782.5 4.8 copy-start.1
where the time goes:
time: 798 us; the launch traced here: 788 us
  waiting for transfers between devices  271 us (34%)
  blocking collectives  158 us (20%)
  local copies, waits for them, and re-layouts  145 us (18%)
  matrix products  104 us (13%)
  starting transfers between devices  68 us (9%)
  other arithmetic  41 us (5%)
    all_to_all x2, waiting for transfers between devices, body(): lax.all_to_all(sent_terms, 'bin', split_axis=0, concat_axis=0, tiled=True)  182 us
    unnamed x39, local copies, waits for them, and re-layouts  130 us
    all_to_all x1, blocking collectives, body(): lax.all_to_all(row_refs.reshape(bin_count, cap_first, pixel_count), 'bin'...  99.9 us
    all_to_all x1, waiting for transfers between devices, body(): lax.all_to_all(row_refs.reshape(bin_count, cap_first, pixel_count), 'bin'...  78.8 us
    dot_general x12, matrix products, pick_rows(): jnp.dot(selector.astype(jnp.bfloat16), values, preferred_element_type=jnp...  72.1 us
    all_to_all x2, blocking collectives, body(): lax.all_to_all(ref_rows.reshape(mic_count, cap_second, pixel_count), 'mic...  37.2 us
    dot_general x2, matrix products, accumulate(): jnp.dot(member.astype(jnp.float32), ctf_power, precision=lax.Precision.HI...  22.8 us
    all_to_all x1, blocking collectives, body(): lax.all_to_all(first_labels, 'bin', split_axis=0, concat_axis=0, tiled=True)  20.4 us
  transfers between devices with their start and end apart: 10, of which 6 were waited for; matrix products, arithmetic and copies ran while one was open for 16% of the time, Pallas kernels for 0%

commit v1 on v0

v1 whole, which is shorter than its diff:
```python
import functools
import math

import jax
import jax.numpy as jnp
from jax import lax
from jax.experimental import pallas as pl
from jax.experimental.pallas import tpu as pltpu
from jax.sharding import PartitionSpec as P

ITERS = 2
PRIOR_WEIGHT = 0.5
EPSILON = 1e-06
CONTRAST = 0.1
AMPLITUDE = math.sqrt(1.0 - CONTRAST * CONTRAST)
SIDE = 256
PIXELS = SIDE * SIDE
N_MIC, N_BIN, N_Z, N_Y = 8, 32, 8, 4
OWN, MINE = 8, 4
ROWS = 32


def hartley(side):
    k = lax.broadcasted_iota(jnp.int32, (side, side), 0)
    x = lax.broadcasted_iota(jnp.int32, (side, side), 1)
    angles = (k * x % side).astype(jnp.float32) * (2.0 * math.pi / side)
    return ((jnp.cos(angles) + jnp.sin(angles)) / math.sqrt(side)).astype(jnp.bfloat16)


def transform(images, offsets):
    basis = hartley(SIDE)
    r = lax.broadcasted_iota(jnp.int32, (MINE, SIDE, SIDE), 1)
    c = lax.broadcasted_iota(jnp.int32, (MINE, SIDE, SIDE), 2)
    take_rows = (c == (r + offsets[0][:, None, None]) % SIDE).astype(jnp.bfloat16)
    take_columns = (r == (c + offsets[1][:, None, None]) % SIDE).astype(jnp.bfloat16)
    dot = functools.partial(jnp.einsum, preferred_element_type=jnp.float32)
    moved = dot("prx,pxc->prc", take_rows, images).astype(jnp.bfloat16)
    moved = dot("prx,pxc->prc", moved, take_columns).astype(jnp.bfloat16)
    half = dot("kx,pxy->pky", basis, moved).astype(jnp.bfloat16)
    return dot("pky,ly->pkl", half, basis).astype(jnp.bfloat16)


def refine_kernel(place_ref, valid_ref, group_ref, focus_ref, damp_ref, spectra_ref, refs_ref,
                  out_ref, score_ref, ctf_ref, num_ref, den_ref, weight_ref):
    slot = lax.broadcasted_iota(jnp.int32, (N_MIC, SIDE), 0)
    focus = jnp.zeros((N_MIC, SIDE), jnp.float32)
    damp = jnp.zeros((N_MIC, SIDE), jnp.float32)
    for s in range(N_MIC):
        group = group_ref[s]
        focus = jnp.where(slot == s, focus_ref[group], focus)
        damp = jnp.where(slot == s, damp_ref[group], damp)
    k = lax.broadcasted_iota(jnp.int32, (N_MIC, SIDE), 1)
    folded = jnp.minimum(k, SIDE - k).astype(jnp.float32) / (SIDE / 2.0)
    square = folded * folded
    sine, cosine = jnp.sin(focus * square), jnp.cos(focus * square)
    envelope = jnp.exp(-damp * square)
    row_sine = jnp.transpose(-sine * envelope)
    row_cosine = jnp.transpose(-cosine * envelope)
    col_sine = (AMPLITUDE * cosine - CONTRAST * sine) * envelope
    col_cosine = (AMPLITUDE * sine + CONTRAST * cosine) * envelope
    for s in range(N_MIC):
        ctf_ref[s] = (
            row_sine[:, s : s + 1] * col_sine[s : s + 1, :]
            + row_cosine[:, s : s + 1] * col_cosine[s : s + 1, :]
        )
    out_ref[...] = refs_ref[...]
    score_ref[...] = jnp.zeros_like(score_ref)

    def chunk(i):
        return pl.ds(pl.multiple_of(i * ROWS, ROWS), ROWS)

    def one_place(p, _):
        count = jnp.int32(0)
        for s in range(N_MIC):
            count += jnp.where((place_ref[s] == p) & (valid_ref[s] > 0), 1, 0)

        @pl.when(count > 0)
        def _():
            @pl.loop(0, ITERS)
            def _(iteration):
                num_ref[...] = jnp.zeros_like(num_ref)
                den_ref[...] = jnp.zeros_like(den_ref)

                @pl.loop(0, N_MIC)
                def _(s):
                    @pl.when((place_ref[s] == p) & (valid_ref[s] > 0))
                    def _():
                        def correlate(i, sums):
                            cross, model, data = sums
                            predicted = ctf_ref[s, chunk(i), :] * out_ref[p, chunk(i), :].astype(jnp.float32)
                            values = spectra_ref[s, chunk(i), :].astype(jnp.float32)
                            return (
                                cross + predicted * values,
                                model + predicted * predicted,
                                data + values * values,
                            )

                        zero = jnp.zeros((ROWS, SIDE), jnp.float32)
                        cross, model, data = lax.fori_loop(0, SIDE // ROWS, correlate, (zero, zero, zero))
                        cross = jnp.sum(cross, keepdims=True) / PIXELS
                        model = jnp.sum(model, keepdims=True) / PIXELS + EPSILON
                        data = jnp.sum(data, keepdims=True) / PIXELS + EPSILON
                        correlation = cross / jnp.sqrt(model * data)
                        weight = 1.0 / (1.0 + jnp.exp(-SIDE * correlation))
                        weight = weight.astype(jnp.bfloat16).astype(jnp.float32)
                        score_ref[pl.ds(s, 1), :] = jnp.broadcast_to(correlation, (1, 128))

                        def gather(i, _):
                            table = ctf_ref[s, chunk(i), :]
                            scaled = weight * table
                            values = spectra_ref[s, chunk(i), :].astype(jnp.float32)
                            term = (scaled * values).astype(jnp.bfloat16).astype(jnp.float32)
                            num_ref[chunk(i), :] += term
                            den_ref[chunk(i), :] += scaled * table
                            return 0

                        lax.fori_loop(0, SIDE // ROWS, gather, 0)

                def update(i, _):
                    previous = out_ref[p, chunk(i), :].astype(jnp.float32)
                    top = num_ref[chunk(i), :] + PRIOR_WEIGHT * previous
                    out_ref[p, chunk(i), :] = (top / (den_ref[chunk(i), :] + PRIOR_WEIGHT)).astype(jnp.bfloat16)
                    return 0

                lax.fori_loop(0, SIDE // ROWS, update, 0)

        return 0

    lax.fori_loop(0, OWN, one_place, 0)


def refine(place, valid, group, defocus, bfactor, spectra, references):
    smem = pl.BlockSpec(memory_space=pltpu.SMEM)
    vmem = pl.BlockSpec(memory_space=pltpu.VMEM)
    return pl.pallas_call(
        refine_kernel,
        out_shape=(
            jax.ShapeDtypeStruct((OWN, SIDE, SIDE), jnp.bfloat16),
            jax.ShapeDtypeStruct((N_MIC, 128), jnp.float32),
        ),
        in_specs=[smem] * 5 + [vmem] * 2,
        out_specs=(vmem, vmem),
        scratch_shapes=[
            pltpu.VMEM((N_MIC, SIDE, SIDE), jnp.float32),
            pltpu.VMEM((SIDE, SIDE), jnp.float32),
            pltpu.VMEM((SIDE, SIDE), jnp.float32),
            pltpu.VMEM((N_MIC, 128), jnp.float32),
        ],
        compiler_params=pltpu.CompilerParams(vmem_limit_bytes=24 << 20),
        name="refine",
    )(place, valid, group, defocus, bfactor, spectra, references)


def pick_kernel(index_ref, tile_ref, out_ref):
    out_ref[...] = tile_ref[...]


def pick(tiles, index):
    return pl.pallas_call(
        pick_kernel,
        out_shape=jax.ShapeDtypeStruct((index.shape[0], SIDE, SIDE), tiles.dtype),
        grid_spec=pltpu.PrefetchScalarGridSpec(
            num_scalar_prefetch=1,
            grid=(index.shape[0],),
            in_specs=[pl.BlockSpec((1, SIDE, SIDE), lambda i, index: (index[i], 0, 0))],
            out_specs=pl.BlockSpec((1, SIDE, SIDE), lambda i, index: (i, 0, 0)),
        ),
        name="pick",
    )(index, tiles)


def body(images, offsets, ctf_group, particle_bin, bin_place, defocus, bfactor, references):
    mic, column = lax.axis_index("mic"), lax.axis_index("bin")
    my_y, my_z = column % N_Y, column // N_Y
    places = jnp.take(bin_place, particle_bin)
    labels = lax.all_gather(jnp.stack([places, ctf_group]), ("mic", "bin"))
    place_of = labels[:, 0].reshape(N_MIC, N_BIN * MINE)
    group_of = labels[:, 1].reshape(N_MIC, N_BIN * MINE)
    spectra = transform(images, offsets)

    lines = [[z * N_Y + y for z in range(N_Z)] for y in range(N_Y)]
    line = lax.all_gather(spectra, "bin", axis_index_groups=lines).reshape(N_Z * MINE, SIDE, SIDE)
    row = jnp.take(place_of, mic, axis=0).reshape(N_Z, N_Y, MINE)
    owner = row // OWN
    to_mic, to_z, to_y = owner // N_BIN, owner % N_BIN // N_Y, owner % N_Y
    line_z = jnp.take(to_z, my_y, axis=1).reshape(N_Z * MINE)
    line_y = jnp.take(to_y, my_y, axis=1).reshape(N_Z * MINE)
    order = jnp.arange(N_Z * MINE)
    for_y = (line_z == my_z)[None, :] & (line_y[None, :] == jnp.arange(N_Y)[:, None])
    rank = jnp.sum(for_y[:, None, :] & (order[None, :] < order[:, None])[None], axis=2)
    first = for_y[:, None, :] & (rank[:, None, :] == jnp.arange(MINE)[None, :, None])
    first = jnp.sum(first * order, axis=2)
    packed = pick(line, first.reshape(N_Y * MINE)).reshape(N_Y, MINE, SIDE, SIDE)
    planes = [[z * N_Y + y for y in range(N_Y)] for z in range(N_Z)]
    plane = lax.all_to_all(packed, "bin", 0, 0, axis_index_groups=planes, tiled=True)
    plane = plane.reshape(N_Y * MINE, SIDE, SIDE)
    here = (to_z == my_z) & (to_y == my_y)
    here_line = jnp.transpose(here, (1, 0, 2)).reshape(N_Y, N_Z * MINE)
    mic_line = jnp.transpose(to_mic, (1, 0, 2)).reshape(N_Y, N_Z * MINE)
    rank = jnp.sum(here_line[:, None, :] & (order[None, :] < order[:, None])[None], axis=2)
    position = jnp.arange(N_Y)[:, None] * MINE + rank
    chosen = here_line[None] & (mic_line[None] == jnp.arange(N_MIC)[:, None, None])
    second = jnp.sum(chosen * position[None], axis=(1, 2))
    sent = pick(plane, second)
    owned = lax.all_to_all(sent, "mic", 0, 0, tiled=True)

    mine = place_of // OWN == mic * N_BIN + column
    valid = jnp.sum(mine, axis=1).astype(jnp.int32)
    place = jnp.sum(mine * (place_of % OWN), axis=1)
    group = jnp.sum(mine * group_of, axis=1)
    refined, correlations = refine(place, valid, group, defocus, bfactor, owned, references)
    every = lax.all_gather(correlations[:, 0], ("mic", "bin"))
    scores = jnp.take(every.reshape(-1), places // OWN * N_MIC + mic)
    return (refined, scores)


def solution(mesh):
    tiles, items = P(("mic", "bin"), None, None), P(("mic", "bin"))
    return jax.shard_map(
        body,
        mesh=mesh,
        in_specs=(tiles, P(None, ("mic", "bin")), items, items, P(), P(), P(), tiles),
        out_specs=(tiles, items),
        check_vma=False,
    )
```

time: 798 us -> 256 us (0.32); the launches traced: 788 us -> 255 us
  waiting for transfers between devices: 271 us -> 37 us
  local copies, waits for them, and re-layouts: 145 us -> 5.65 us
  matrix products: 104 us -> 3.34 us
  starting transfers between devices: 68 us -> 11 us
  other arithmetic: 41 us -> 17.2 us
  Pallas kernels: 0 us -> 22.6 us
  blocking collectives: 158 us -> 144 us
  between operations: 1.42 us -> 14.3 us
    all_to_all x10 -> x2, waiting for transfers between devices: 271 us -> 37 us  [the longest x1 22.5 us: body(): lax.all_to_all(packed, 'bin', 0, 0, axis_index_groups=planes, tiled=True)]
    all_to_all x4 -> x0, blocking collectives: 158 us -> none  [the longest x1 99.9 us: body(): lax.all_to_all(row_refs.reshape(bin_count, cap_first, pixel_count), 'bin'...]
    unnamed x39 -> x18, local copies, waits for them, and re-layouts: 130 us -> 1.93 us
    dot_general x17 -> x2, matrix products: 104 us -> 3.34 us  [the longest x1 2.52 us: transform(): return dot('pky,ly->pkl', half, basis).astype(jnp.bfloat16)]
    reshape x0 -> x1, blocking collectives: none -> 75.2 us  [body(): scores = jnp.take(every.reshape(-1), places // OWN * N_MIC + mic)]
    all_gather x0 -> x1, blocking collectives: none -> 69.2 us  [body(): labels = lax.all_gather(jnp.stack([places, ctf_group]), ('mic', 'bin'))]
    all_to_all x10 -> x2, starting transfers between devices: 68 us -> 11 us  [the longest x1 7.37 us: body(): owned = lax.all_to_all(sent, 'mic', 0, 0, tiled=True)]
    reshape x10 -> x0, other arithmetic: 33.5 us -> none  [the longest x2 13.7 us: body(): pick_rows(first_pick, weighted).reshape(bin_count, cap_first, pixel_count)]
  transfers between devices with their start and end apart: 10 -> 3, of which waited for: 6 -> 2; matrix products, arithmetic and copies ran while one was open for 16% -> 7% of each run, Pallas kernels for 0% -> 0%
where the time goes in v1:
time: 256 us; the launch traced here: 255 us
  blocking collectives  144 us (56%)
  waiting for transfers between devices  37 us (14%)
  Pallas kernels  22.6 us (9%)
  other arithmetic  17.2 us (7%)
  between operations  14.3 us (6%)
  starting transfers between devices  11 us (4%)
  local copies, waits for them, and re-layouts  5.65 us (2%)
  matrix products  3.34 us (1%)
    reshape x1, blocking collectives, body(): scores = jnp.take(every.reshape(-1), places // OWN * N_MIC + mic)  75.2 us
    all_gather x1, blocking collectives, body(): labels = lax.all_gather(jnp.stack([places, ctf_group]), ('mic', 'bin'))  69.2 us
    all_to_all x1, waiting for transfers between devices, body(): lax.all_to_all(packed, 'bin', 0, 0, axis_index_groups=planes, tiled=True)  22.5 us
    all_to_all x1, waiting for transfers between devices, body(): owned = lax.all_to_all(sent, 'mic', 0, 0, tiled=True)  14.5 us
    slice x1, other arithmetic, body(): place_of = labels[:, 0].reshape(N_MIC, N_BIN * MINE)  14.3 us
    pallas_call x2, Pallas kernels, pick(): pl.pallas_call(pick_kernel, out_shape=jax.ShapeDtypeStruct((index.shape[0...  14.1 us
    pallas_call x1, Pallas kernels, refine(): pl.pallas_call(refine_kernel, out_shape=(jax.ShapeDtypeStruct((OWN, SIDE,...  8.47 us
    all_to_all x1, starting transfers between devices, body(): owned = lax.all_to_all(sent, 'mic', 0, 0, tiled=True)  7.37 us
  transfers between devices with their start and end apart: 3, of which 2 were waited for; matrix products, arithmetic and copies ran while one was open for 7% of the time, Pallas kernels for 0%

profile of v1, /device:TPU:1, one launch (start us, length us, event | category | flops | bytes accessed | tf_op | source)
XLA Modules:
  0.0 255.5 jit_solution(7548136245467809860)
XLA Ops:
  7.2 0.8 slice_bitcast_fusion.1
  8.0 0.3 copy-done
  8.2 0.8 convolution_convert_fusion.2
  9.1 2.5 convolution_convert_fusion
  11.7 0.6 gather_fusion
  12.4 69.2 %all-gather.3 = s32[256,2,4]{2,1,0:T(2,128)S(1)} all-gather(s32[1,2,4]{2,1,0:T(2,128)S(1)} %add_bitcast_fusion), channel_id=2, replica_groups=mesh['mic'=8,'bin'=32] {'mic','bin'}, dimensions={0}, use_global_device_ids=true | all-gather | bytes 8224 | tf_op jit(solution)/shard_map/all_gather | solution.py:176
  81.6 0.7 fusion.51
  82.3 14.3 %slice_reduce_fusion = (s32[256,4]{1,0:T(8,128)S(1)}, s32[256]{0:T(256)S(1)}, s32[256]{0:T(256)S(1)}, s32[256]{0:T(256)S(1)}) fusion(s32[256,2,4]{2,1,0:T(2,128)S(1)} %all-gather.3, pred[256,1,4]{2,1,0:T(4,128)(4,1)S(1)} %get-tuple-element.40, s32[256,1,4]{2,1,0:T(1,128)S(1)} %get-tuple-element.41), kind=kLoop, calls=%fused_computation.92 | loop fusion | flops 10496 | bytes 20480 | tf_op jit(solution)/shard_map/slice | solution.py:177
  97.5 0.2 convert_reduce_fusion.1
  97.7 0.1 select_reduce_fusion.1
  97.9 0.6 reshape.142.index_ref
  98.5 8.1 %pick.2 = bf16[16,256,256]{2,1,0:T(8,128)(2,1)} custom-call(s32[16]{0:T(128)} %reshape.142.index_ref, bf16[32,256,256]{2,1,0:T(8,128)(2,1)} %all-gather.6.cloned.1.call-done.tile_ref), custom_call_target="tpu_custom_call" | custom-call | tf_op jit(solution)/shard_map/pick/pallas_call | solution.py:159
  106.6 3.6 %all-to-all-start = ((bf16[4,4,256,256]{3,2,1,0:T(8,128)(2,1)}), bf16[4,4,256,256]{3,2,1,0:T(8,128)(2,1)S(1)}, u32[]{:S(2)}, u32[]{:S(2)}) async-start(bf16[4,4,256,256]{3,2,1,0:T(8,128)(2,1)} %bitcast.28), calls=%async_computation | async-start | bytes 4194304 | tf_op jit(solution)/shard_map/all_to_all | solution.py:195
  110.4 0.6 select_reduce_fusion.index_ref
  111.1 22.5 %all-to-all-done = bf16[4,4,256,256]{3,2,1,0:T(8,128)(2,1)S(1)} async-done(((bf16[4,4,256,256]{3,2,1,0:T(8,128)(2,1)}), bf16[4,4,256,256]{3,2,1,0:T(8,128)(2,1)S(1)}, u32[]{:S(2)}, u32[]{:S(2)}) %all-to-all-start) | async-done | bytes 2097184 | tf_op jit(solution)/shard_map/all_to_all | solution.py:195
  133.5 1.3 copy-done.5
  134.9 6.0 %pick.3 = bf16[8,256,256]{2,1,0:T(8,128)(2,1)} custom-call(s32[8]{0:T(128)} %select_reduce_fusion.index_ref, bf16[16,256,256]{2,1,0:T(8,128)(2,1)} %bitcast.29), custom_call_target="tpu_custom_call" | custom-call | tf_op jit(solution)/shard_map/pick/pallas_call | solution.py:159
  140.9 7.4 %all-to-all-start.1 = ((bf16[8,256,256]{2,1,0:T(8,128)(2,1)}), bf16[8,256,256]{2,1,0:T(8,128)(2,1)S(1)}, u32[]{:S(2)}, u32[]{:S(2)}) async-start(bf16[8,256,256]{2,1,0:T(8,128)(2,1)} %pick.3), calls=%async_computation.1 | async-start | bytes 2097152 | tf_op jit(solution)/shard_map/all_to_all | solution.py:205
  148.9 14.5 %all-to-all-done.1.spectra_ref = bf16[8,256,256]{2,1,0:T(8,128)(2,1)S(1)} async-done(((bf16[8,256,256]{2,1,0:T(8,128)(2,1)}), bf16[8,256,256]{2,1,0:T(8,128)(2,1)S(1)}, u32[]{:S(2)}, u32[]{:S(2)}) %all-to-all-start.1) | async-done | bytes 1048608 | tf_op jit(solution)/shard_map/all_to_all | solution.py:205
  163.4 8.5 %refine.1 = (bf16[8,256,256]{2,1,0:T(8,128)(2,1)}, f32[8,128]{1,0:T(8,128)S(1)}) custom-call(s32[8]{0:T(128)S(1)} %reduce_sum.86.place_ref, s32[8]{0:T(128)S(1)} %reduce_sum.89.valid_ref, s32[8]{0:T(128)S(1)} %reduce_sum.92.group_ref, f32[64]{0:T(128)S(1)} %copy-done.2, f32[64]{0:T(128)S(1)} %copy-done.3, ...), custom_call_target="tpu_custom_call" | custom-call | tf_op jit(solution)/shard_map/refine/pallas_call | solution.py:135
  171.9 0.3 dynamic-update-slice.2
  172.2 75.2 %all-reduce = f32[2048]{0:T(1024)S(1)} all-reduce(f32[2048]{0:T(1024)S(1)} %dynamic-update-slice.2), channel_id=4, replica_groups=mesh['mic'=8,'bin'=32] {'mic','bin'}, use_global_device_ids=true, to_apply=%add | all-reduce | flops 2048 | bytes 16384 | tf_op jit(solution)/shard_map/reshape | solution.py:213
  247.5 0.6 gather_fusion.1
  248.1 0.5 and_select_fusion.2
  (49 shorter events, 1.8 us)
Async XLA Ops:
  7.2 1.1 copy-start
  7.2 91.3 %all-gather.6.cloned.1.call-start = ((), (), s32[]{:S(2)}) async-start(), calls=%async_computation.2 | async-start | bytes 4718592 | tf_op jit(solution)/shard_map/all_gather | solution.py:182
  9.1 2.6 %copy-start.6 = (s32[4]{0:T(128)S(1)}, s32[4]{0:T(128)}, u32[]{:S(2)}) copy-start(s32[4]{0:T(128)} %param.13) | copy-start | bytes 52
  9.1 2.6 %copy-start.4 = (s32[2048]{0:T(1024)S(1)}, s32[2048]{0:T(1024)}, u32[]{:S(2)}) copy-start(s32[2048]{0:T(1024)} %param.14) | copy-start | bytes 24580
  9.1 3.3 %copy-start.7 = (s32[4]{0:T(128)S(1)}, s32[4]{0:T(128)}, u32[]{:S(2)}) copy-start(s32[4]{0:T(128)} %param.12) | copy-start | bytes 52
  106.6 26.9 %all-to-all-start = ((bf16[4,4,256,256]{3,2,1,0:T(8,128)(2,1)}), bf16[4,4,256,256]{3,2,1,0:T(8,128)(2,1)S(1)}, u32[]{:S(2)}, u32[]{:S(2)}) async-start(bf16[4,4,256,256]{3,2,1,0:T(8,128)(2,1)} %bitcast.28), calls=%async_computation | async-start | bytes 4194304 | tf_op jit(solution)/shard_map/all_to_all | solution.py:195
  133.5 1.4 copy-start.5
  134.9 28.5 %copy-start.1 = (bf16[8,256,256]{2,1,0:T(8,128)(2,1)S(1)}, bf16[8,256,256]{2,1,0:T(8,128)(2,1)}, u32[]{:S(2)}) copy-start(bf16[8,256,256]{2,1,0:T(8,128)(2,1)} %refs_ref.1) | copy-start | bytes 3145732
  134.9 28.5 %copy-start.2 = (f32[64]{0:T(128)S(1)}, f32[64]{0:T(128)}, u32[]{:S(2)}) copy-start(f32[64]{0:T(128)} %focus_ref.1) | copy-start | bytes 772
  134.9 28.5 %copy-start.3 = (f32[64]{0:T(128)S(1)}, f32[64]{0:T(128)}, u32[]{:S(2)}) copy-start(f32[64]{0:T(128)} %damp_ref.1) | copy-start | bytes 772
  140.9 22.5 %all-to-all-start.1 = ((bf16[8,256,256]{2,1,0:T(8,128)(2,1)}), bf16[8,256,256]{2,1,0:T(8,128)(2,1)S(1)}, u32[]{:S(2)}, u32[]{:S(2)}) async-start(bf16[8,256,256]{2,1,0:T(8,128)(2,1)} %pick.3), calls=%async_computation.1 | async-start | bytes 2097152 | tf_op jit(solution)/shard_map/all_to_all | solution.py:205
Sparse Core Ops, SparseCore 0:
  11.8 59.8 all-gather.5

commit v2 on v1

v2 whole, which is shorter than its diff:
```python
import functools
import math

import jax
import jax.numpy as jnp
from jax import lax
from jax.experimental import pallas as pl
from jax.experimental.pallas import tpu as pltpu
from jax.sharding import PartitionSpec as P

ITERS = 2
PRIOR_WEIGHT = 0.5
EPSILON = 1e-06
CONTRAST = 0.1
AMPLITUDE = math.sqrt(1.0 - CONTRAST * CONTRAST)
SIDE = 256
PIXELS = SIDE * SIDE
N_MIC, N_BIN, N_Z, N_Y = 8, 32, 8, 4
OWN, MINE = 8, 4
ROWS = 32
CTF_GROUPS = 64
CHUNKS = 4
DEPTH = SIDE // CHUNKS
MESH = pl.DeviceIdType.MESH


def hartley(side):
    k = lax.broadcasted_iota(jnp.int32, (side, side), 0)
    x = lax.broadcasted_iota(jnp.int32, (side, side), 1)
    angles = (k * x % side).astype(jnp.float32) * (2.0 * math.pi / side)
    return ((jnp.cos(angles) + jnp.sin(angles)) / math.sqrt(side)).astype(jnp.bfloat16)


def transform(images, offsets):
    basis = hartley(SIDE)
    r = lax.broadcasted_iota(jnp.int32, (MINE, SIDE, SIDE), 1)
    c = lax.broadcasted_iota(jnp.int32, (MINE, SIDE, SIDE), 2)
    take_rows = (c == (r + offsets[0][:, None, None]) % SIDE).astype(jnp.bfloat16)
    take_columns = (r == (c + offsets[1][:, None, None]) % SIDE).astype(jnp.bfloat16)
    dot = functools.partial(jnp.einsum, preferred_element_type=jnp.float32)
    moved = dot("prx,pxc->prc", take_rows, images).astype(jnp.bfloat16)
    moved = dot("prx,pxc->prc", moved, take_columns).astype(jnp.bfloat16)
    half = dot("kx,pxy->pky", basis, moved).astype(jnp.bfloat16)
    return dot("pky,ly->pkl", half, basis).astype(jnp.bfloat16)


def refine_kernel(label_ref, focus_ref, damp_ref, spectra_ref, refs_ref,
                  out_ref, score_ref, ctf_ref, num_ref, den_ref):
    slot = lax.broadcasted_iota(jnp.int32, (N_MIC, SIDE), 0)
    focus = jnp.zeros((N_MIC, SIDE), jnp.float32)
    damp = jnp.zeros((N_MIC, SIDE), jnp.float32)
    for s in range(N_MIC):
        group = (label_ref[s, 0] - 1) & (CTF_GROUPS - 1)
        focus = jnp.where(slot == s, focus_ref[group], focus)
        damp = jnp.where(slot == s, damp_ref[group], damp)
    k = lax.broadcasted_iota(jnp.int32, (N_MIC, SIDE), 1)
    folded = jnp.minimum(k, SIDE - k).astype(jnp.float32) / (SIDE / 2.0)
    square = folded * folded
    sine, cosine = jnp.sin(focus * square), jnp.cos(focus * square)
    envelope = jnp.exp(-damp * square)
    row_sine = jnp.transpose(-sine * envelope)
    row_cosine = jnp.transpose(-cosine * envelope)
    col_sine = (AMPLITUDE * cosine - CONTRAST * sine) * envelope
    col_cosine = (AMPLITUDE * sine + CONTRAST * cosine) * envelope
    for s in range(N_MIC):
        ctf_ref[s] = (
            row_sine[:, s : s + 1] * col_sine[s : s + 1, :]
            + row_cosine[:, s : s + 1] * col_cosine[s : s + 1, :]
        )
    out_ref[...] = refs_ref[...]
    score_ref[...] = jnp.zeros_like(score_ref)

    def chunk(i):
        return pl.ds(pl.multiple_of(i * ROWS, ROWS), ROWS)

    def kept_at(s, p):
        code = label_ref[s, 0]
        return (code > 0) & ((((code - 1) >> 6) & (OWN - 1)) == p)

    def one_place(p, _):
        count = jnp.int32(0)
        for s in range(N_MIC):
            count += jnp.where(kept_at(s, p), 1, 0)

        @pl.when(count > 0)
        def _():
            @pl.loop(0, ITERS)
            def _(iteration):
                num_ref[...] = jnp.zeros_like(num_ref)
                den_ref[...] = jnp.zeros_like(den_ref)

                @pl.loop(0, N_MIC)
                def _(s):
                    @pl.when(kept_at(s, p))
                    def _():
                        def correlate(i, sums):
                            cross, model, data = sums
                            predicted = ctf_ref[s, chunk(i), :] * out_ref[p, chunk(i), :].astype(jnp.float32)
                            values = spectra_ref[s, chunk(i), :].astype(jnp.float32)
                            return (
                                cross + predicted * values,
                                model + predicted * predicted,
                                data + values * values,
                            )

                        zero = jnp.zeros((ROWS, SIDE), jnp.float32)
                        cross, model, data = lax.fori_loop(0, SIDE // ROWS, correlate, (zero, zero, zero))
                        cross = jnp.sum(cross, keepdims=True) / PIXELS
                        model = jnp.sum(model, keepdims=True) / PIXELS + EPSILON
                        data = jnp.sum(data, keepdims=True) / PIXELS + EPSILON
                        correlation = cross / jnp.sqrt(model * data)
                        weight = 1.0 / (1.0 + jnp.exp(-SIDE * correlation))
                        weight = weight.astype(jnp.bfloat16).astype(jnp.float32)
                        score_ref[s] = jnp.broadcast_to(correlation, (8, 128))

                        def gather(i, _):
                            table = ctf_ref[s, chunk(i), :]
                            scaled = weight * table
                            values = spectra_ref[s, chunk(i), :].astype(jnp.float32)
                            term = (scaled * values).astype(jnp.bfloat16).astype(jnp.float32)
                            num_ref[chunk(i), :] += term
                            den_ref[chunk(i), :] += scaled * table
                            return 0

                        lax.fori_loop(0, SIDE // ROWS, gather, 0)

                def update(i, _):
                    previous = out_ref[p, chunk(i), :].astype(jnp.float32)
                    top = num_ref[chunk(i), :] + PRIOR_WEIGHT * previous
                    out_ref[p, chunk(i), :] = (top / (den_ref[chunk(i), :] + PRIOR_WEIGHT)).astype(jnp.bfloat16)
                    return 0

                lax.fori_loop(0, SIDE // ROWS, update, 0)

        return 0

    lax.fori_loop(0, OWN, one_place, 0)


def refine(labels, defocus, bfactor, spectra, references):
    smem = pl.BlockSpec(memory_space=pltpu.SMEM)
    vmem = pl.BlockSpec(memory_space=pltpu.VMEM)
    return pl.pallas_call(
        refine_kernel,
        out_shape=(
            jax.ShapeDtypeStruct((OWN, SIDE, SIDE), jnp.bfloat16),
            jax.ShapeDtypeStruct((N_MIC, 8, 128), jnp.float32),
        ),
        in_specs=[smem] * 3 + [vmem] * 2,
        out_specs=(vmem, vmem),
        scratch_shapes=[
            pltpu.VMEM((N_MIC, SIDE, SIDE), jnp.float32),
            pltpu.VMEM((SIDE, SIDE), jnp.float32),
            pltpu.VMEM((SIDE, SIDE), jnp.float32),
        ],
        compiler_params=pltpu.CompilerParams(vmem_limit_bytes=24 << 20),
        name="refine",
    )(labels, defocus, bfactor, spectra, references)


def code_of(bin_ref, place_ref, group_ref, j):
    return place_ref[bin_ref[j]] * CTF_GROUPS + group_ref[j] + 1


def meet(peers):
    barrier = pltpu.get_barrier_semaphore()
    for peer in peers:
        pl.semaphore_signal(barrier, inc=1, device_id=peer, device_id_type=MESH)
    pl.semaphore_wait(barrier, len(peers))


def lanes_of(values):
    lane = lax.broadcasted_iota(jnp.int32, (8, 128), 1)
    tile = jnp.zeros((8, 128), jnp.int32)
    for j, value in enumerate(values):
        tile = jnp.where(lane == j, value, tile)
    return tile


def route_kernel(bin_ref, bin_place_ref, group_ref, spectra_ref, out_ref, label_ref, *scratch):
    lines, packs = scratch[:CHUNKS], scratch[CHUNKS : 2 * CHUNKS]
    planes, parcels = scratch[2 * CHUNKS : 3 * CHUNKS], scratch[3 * CHUNKS : 4 * CHUNKS]
    (line_label, pack_label, plane_label, parcel_label, mine_label, line_code, plane_code,
     z_send, z_recv, y_send, y_recv, m_send, m_recv, zl_send, zl_recv, yl_send, yl_recv,
     ml_send, ml_recv, code_sem) = scratch[4 * CHUNKS :]
    mic, column = lax.axis_index("mic"), lax.axis_index("bin")
    z, y = column // N_Y, lax.rem(column, N_Y)

    def at_z(d):
        return (mic, lax.rem(z + d, N_Z) * N_Y + y)

    def at_y(d):
        return (mic, z * N_Y + lax.rem(y + d, N_Y))

    def at_mic(d):
        return (lax.rem(mic + d, N_MIC), column)

    def send(src, dst, send_sem, recv_sem, peer):
        copy = pltpu.make_async_remote_copy(
            src_ref=src, dst_ref=dst, send_sem=send_sem, recv_sem=recv_sem,
            device_id=peer, device_id_type=MESH,
        )
        copy.start()
        copies.append(copy)
        return copy

    copies = []
    meet([at_z(d) for d in range(1, N_Z)] + [at_y(d) for d in range(1, N_Y)] + [at_mic(d) for d in range(1, N_MIC)])

    line_label[0] = lanes_of([code_of(bin_ref, bin_place_ref, group_ref, j) for j in range(MINE)])
    line_labels = [
        send(line_label.at[0], line_label.at[N_Z - d], zl_send.at[d - 1], zl_recv.at[d - 1], at_z(d))
        for d in range(1, N_Z)
    ]
    hops, y_copies, m_copies = {}, {}, {}
    pick_line, pick_plane = [], []
    half = N_Z // 2

    def hop(c, h):
        line = lines[c]
        if h == 1:
            line[0:MINE] = spectra_ref[:, c * DEPTH : (c + 1) * DEPTH, :]
        for way in range(2):
            if h > 1:
                hops[c, way, h - 1].wait_recv()
            src = lax_mod(1 - h, N_Z) if way == 0 else h - 1
            dst = N_Z - h if way == 0 else h
            low, count = 0, MINE
            if h == half:
                low, count = (MINE // 2) * way, MINE // 2
            hops[c, way, h] = send(
                line.at[pl.ds(src * MINE + low, count)], line.at[pl.ds(dst * MINE + low, count)],
                z_send.at[c, way, h - 1], z_recv.at[c, way, h - 1], at_z(1 if way == 0 else N_Z - 1),
            )

    def choose_line():
        for copy in line_labels:
            copy.wait_recv()
        fetch = pltpu.make_async_copy(line_label, line_code, code_sem.at[0])
        fetch.start()
        fetch.wait()
        keys = [[jnp.int32(0)] * MINE for _ in range(N_Y)]
        counts = [jnp.int32(0)] * N_Y
        for t in range(N_Z * MINE):
            code = line_code[t // MINE, 0, t % MINE]
            owner = (code - 1) >> 9
            here = ((owner >> 2) & (N_Z - 1)) == z
            away = (owner - y) & (N_Y - 1)
            key = code * (N_Z * MINE) + t
            for d in range(N_Y):
                hit = here & (away == d)
                rank = jnp.where(hit, counts[d], MINE)
                counts[d] = counts[d] + jnp.where(hit, 1, 0)
                keys[d] = [jnp.where(rank == k, key, keys[d][k]) for k in range(MINE)]
        pick_line.extend([[key & (N_Z * MINE - 1) for key in keys[d]] for d in range(N_Y)])
        for d in range(N_Y):
            tile = lanes_of([key >> 5 for key in keys[d]])
            if d == 0:
                plane_label[0] = tile
            else:
                pack_label[d - 1] = tile

    def to_plane(c):
        for way in range(2):
            hops[c, way, half].wait_recv()
        for d in range(N_Y):
            for k in range(MINE):
                tile = lines[c][pick_line[d][k]]
                if d == 0:
                    planes[c][k] = tile
                else:
                    packs[c][(d - 1) * MINE + k] = tile
        for d in range(1, N_Y):
            y_copies[c, d] = send(
                packs[c].at[pl.ds((d - 1) * MINE, MINE)], planes[c].at[pl.ds((N_Y - d) * MINE, MINE)],
                y_send.at[c, d - 1], y_recv.at[c, d - 1], at_y(d),
            )

    def choose_plane():
        fetch = pltpu.make_async_copy(plane_label, plane_code, code_sem.at[1])
        fetch.start()
        fetch.wait()
        keys = [jnp.int32(0)] * N_MIC
        for s in range(N_Y * MINE):
            code = plane_code[s // MINE, 0, s % MINE]
            away = (((code - 1) >> 14) - mic) & (N_MIC - 1)
            away = jnp.where(code > 0, away, N_MIC)
            key = code * (N_Y * MINE) + s
            keys = [jnp.where(away == d, key, keys[d]) for d in range(N_MIC)]
        pick_plane.extend([key & (N_Y * MINE - 1) for key in keys])
        for d in range(N_MIC):
            tile = jnp.full((8, 128), keys[d] >> 4, jnp.int32)
            if d == 0:
                mine_label[0] = tile
            else:
                parcel_label[d - 1] = tile

    def to_owner(c):
        for d in range(1, N_Y):
            y_copies[c, d].wait_recv()
        rows = pl.ds(c * DEPTH, DEPTH)
        for d in range(N_MIC):
            tile = planes[c][pick_plane[d]]
            if d == 0:
                out_ref[0, rows, :] = tile
            else:
                parcels[c][d - 1] = tile
        for d in range(1, N_MIC):
            m_copies[c, d] = send(
                parcels[c].at[d - 1], out_ref.at[N_MIC - d, rows, :],
                m_send.at[c, d - 1], m_recv.at[c, d - 1], at_mic(d),
            )

    plane_labels, mine_labels = [], []
    for step in range(1, 2 * CHUNKS + half + 3):
        for c in range(CHUNKS):
            h = step - 2 * c
            if 1 <= h <= half:
                hop(c, h)
            elif h == half + 1:
                if c == 0:
                    choose_line()
                    plane_labels += [
                        send(pack_label.at[d - 1], plane_label.at[N_Y - d], yl_send.at[d - 1], yl_recv.at[d - 1], at_y(d))
                        for d in range(1, N_Y)
                    ]
                to_plane(c)
            elif h == half + 3:
                if c == 0:
                    for copy in plane_labels:
                        copy.wait_recv()
                    choose_plane()
                    mine_labels += [
                        send(parcel_label.at[d - 1], mine_label.at[N_MIC - d], ml_send.at[d - 1], ml_recv.at[d - 1], at_mic(d))
                        for d in range(1, N_MIC)
                    ]
                to_owner(c)
    for copy in mine_labels:
        copy.wait_recv()
    for d in range(N_MIC):
        label_ref[pl.ds(d, 1), :] = mine_label[d, 0:1, :]
    for copy in m_copies.values():
        copy.wait_recv()
    for copy in copies:
        copy.wait_send()


def lax_mod(a, n):
    return a % n


def route(particle_bin, bin_place, ctf_group, spectra):
    smem = pl.BlockSpec(memory_space=pltpu.SMEM)
    vmem = pl.BlockSpec(memory_space=pltpu.VMEM)
    buffers = [pltpu.VMEM((n, DEPTH, SIDE), jnp.bfloat16)
               for n in (N_Z * MINE, (N_Y - 1) * MINE, N_Y * MINE, N_MIC - 1) for _ in range(CHUNKS)]
    labels = [pltpu.VMEM((n, 8, 128), jnp.int32) for n in (N_Z, N_Y - 1, N_Y, N_MIC - 1, N_MIC)]
    codes = [pltpu.SMEM((n, 8, 128), jnp.int32) for n in (N_Z, N_Y)]
    dma = pltpu.SemaphoreType.DMA
    sems = [dma(shape) for shape in ((CHUNKS, 2, N_Z // 2), (CHUNKS, N_Y - 1), (CHUNKS, N_MIC - 1),
                                     (N_Z - 1,), (N_Y - 1,), (N_MIC - 1,)) for _ in range(2)]
    return pl.pallas_call(
        route_kernel,
        out_shape=(
            jax.ShapeDtypeStruct((N_MIC, SIDE, SIDE), jnp.bfloat16),
            jax.ShapeDtypeStruct((N_MIC, 128), jnp.int32),
        ),
        in_specs=[smem] * 3 + [vmem],
        out_specs=(vmem, vmem),
        scratch_shapes=buffers + labels + codes + sems + [dma((2,))],
        compiler_params=pltpu.CompilerParams(
            collective_id=0, has_side_effects=True, vmem_limit_bytes=24 << 20
        ),
        name="route",
    )(particle_bin, bin_place, ctf_group, spectra)


def answer_kernel(bin_ref, bin_place_ref, score_ref, out_ref, row, column_scores, m_send, m_recv, b_send, b_recv):
    mic, column = lax.axis_index("mic"), lax.axis_index("bin")
    at_mic = [(lax.rem(mic + d, N_MIC), column) for d in range(N_MIC)]
    at_bin = [(mic, lax.rem(column + d, N_BIN)) for d in range(N_BIN)]
    meet(at_mic[1:] + at_bin[1:])
    copies = []
    for d in range(1, N_MIC):
        copies.append(pltpu.make_async_remote_copy(
            src_ref=score_ref.at[d], dst_ref=row.at[N_MIC - d], send_sem=m_send.at[d - 1],
            recv_sem=m_recv.at[d - 1], device_id=at_mic[d], device_id_type=MESH))
        copies[-1].start()
    row[0] = score_ref[0]
    for copy in copies:
        copy.wait_recv()
    for d in range(N_MIC):
        column_scores[0, pl.ds(d, 1), :] = row[d, 0:1, :]
    spread = []
    for d in range(1, N_BIN):
        spread.append(pltpu.make_async_remote_copy(
            src_ref=column_scores.at[0], dst_ref=column_scores.at[N_BIN - d], send_sem=b_send.at[d - 1],
            recv_sem=b_recv.at[d - 1], device_id=at_bin[d], device_id_type=MESH))
        spread[-1].start()
    for copy in spread:
        copy.wait_recv()
    lane = lax.broadcasted_iota(jnp.int32, (8, 128), 1)
    scores = jnp.zeros((8, 128), jnp.float32)
    for j in range(MINE):
        owner = bin_place_ref[bin_ref[j]] // OWN
        r = (owner - column) & (N_BIN - 1)
        q = ((owner >> 5) - mic) & (N_MIC - 1)
        scores = jnp.where(lane == j, column_scores[r, pl.ds(q, 1), :], scores)
    out_ref[...] = scores
    for copy in copies + spread:
        copy.wait_send()


def answer(particle_bin, bin_place, correlations):
    smem = pl.BlockSpec(memory_space=pltpu.SMEM)
    vmem = pl.BlockSpec(memory_space=pltpu.VMEM)
    dma = pltpu.SemaphoreType.DMA
    return pl.pallas_call(
        answer_kernel,
        out_shape=jax.ShapeDtypeStruct((8, 128), jnp.float32),
        in_specs=[smem, smem, vmem],
        out_specs=vmem,
        scratch_shapes=[
            pltpu.VMEM((N_MIC, 8, 128), jnp.float32),
            pltpu.VMEM((N_BIN, 8, 128), jnp.float32),
            dma((N_MIC - 1,)), dma((N_MIC - 1,)), dma((N_BIN - 1,)), dma((N_BIN - 1,)),
        ],
        compiler_params=pltpu.CompilerParams(collective_id=1, has_side_effects=True),
        name="answer",
    )(particle_bin, bin_place, correlations)


def body(images, offsets, ctf_group, particle_bin, bin_place, defocus, bfactor, references):
    spectra = transform(images, offsets)
    owned, labels = route(particle_bin, bin_place, ctf_group, spectra)
    refined, correlations = refine(labels, defocus, bfactor, owned, references)
    scores = answer(particle_bin, bin_place, correlations)
    return (refined, scores[0, :MINE])


def solution(mesh):
    tiles, items = P(("mic", "bin"), None, None), P(("mic", "bin"))
    return jax.shard_map(
        body,
        mesh=mesh,
        in_specs=(tiles, P(None, ("mic", "bin")), items, items, P(), P(), P(), tiles),
        out_specs=(tiles, items),
        check_vma=False,
    )
```

time: 256 us -> 112 us (0.44)
  blocking collectives: 144 us -> 0 us
  Pallas kernels: 22.6 us -> 105 us
  waiting for transfers between devices: 37 us -> 0 us
  other arithmetic: 17.2 us -> 0 us
  between operations: 14.3 us -> 0.75 us
  starting transfers between devices: 11 us -> 0 us
    pallas_call x2, Pallas kernels: 14.1 us -> 99.9 us  [the longest x1 78.2 us: route(): pl.pallas_call(route_kernel, out_shape=(jax.ShapeDtypeStruct((N_MIC, SIDE...]
    reshape x1 -> x0, blocking collectives: 75.2 us -> none  [body(): scores = jnp.take(every.reshape(-1), places // OWN * N_MIC + mic)]
    all_gather x1 -> x0, blocking collectives: 69.2 us -> none  [body(): labels = lax.all_gather(jnp.stack([places, ctf_group]), ('mic', 'bin'))]
    all_to_all x2 -> x0, waiting for transfers between devices: 37 us -> none  [the longest x1 22.5 us: body(): lax.all_to_all(packed, 'bin', 0, 0, axis_index_groups=planes, tiled=True)]
    slice x1 -> x0, other arithmetic: 14.3 us -> none  [body(): place_of = labels[:, 0].reshape(N_MIC, N_BIN * MINE)]
    all_to_all x2 -> x0, starting transfers between devices: 11 us -> none  [the longest x1 7.37 us: body(): owned = lax.all_to_all(sent, 'mic', 0, 0, tiled=True)]
    pallas_call x1, Pallas kernels: 8.47 us -> 4.93 us  [refine(): pl.pallas_call(refine_kernel, out_shape=(jax.ShapeDtypeStruct((OWN, SIDE,...]
  transfers between devices with their start and end apart: 3 -> 0, of which waited for: 2 -> 0; matrix products, arithmetic and copies ran while one was open for 7% -> 0% of each run, Pallas kernels for 0% -> 0%
where the time goes in v2:
time: 112 us; the launch traced here: 111 us
  Pallas kernels  105 us (94%)
  local copies, waits for them, and re-layouts  3.54 us (3%)
  matrix products  2.28 us (2%)
    pallas_call x1, Pallas kernels, route(): pl.pallas_call(route_kernel, out_shape=(jax.ShapeDtypeStruct((N_MIC, SIDE...  78.2 us
    pallas_call x1, Pallas kernels, answer(): pl.pallas_call(answer_kernel, out_shape=jax.ShapeDtypeStruct((8, 128), jn...  21.6 us
    pallas_call x1, Pallas kernels, refine(): pl.pallas_call(refine_kernel, out_shape=(jax.ShapeDtypeStruct((OWN, SIDE,...  4.93 us

profile of v2, /device:TPU:1, one launch (start us, length us, event | category | flops | bytes accessed | tf_op | source)
XLA Modules:
  0.0 111.4 jit_solution(17469584227946990113)
XLA Ops:
  0.6 0.0 copy-start
  0.6 0.8 slice_bitcast_fusion.2
  1.4 0.3 copy-done
  1.7 0.8 convolution_convert_fusion.2
  2.5 0.0 copy-start.2
  2.5 0.0 copy-start.4
  2.6 0.0 copy-start.5
  2.6 0.0 copy-start.1
  2.6 1.5 %convolution_convert_fusion.1.spectra_ref = bf16[4,256,256]{2,1,0:T(8,128)(2,1)S(1)} fusion(bf16[4,256,256]{2,1,0:T(8,128)(2,1)S(1)} %convolution_convert_fusion.2), kind=kOutput, calls=%fused_computation.7 | convolution fusion | flops 271187968 | bytes 1048576 | tf_op jit(solution)/shard_map/pky,ly->pkl/dot_general | solution.py:44
  4.1 0.0 copy-done.2
  4.1 0.0 copy-done.4
  4.1 0.0 copy-done.5
  4.1 78.2 %route.1 = (bf16[8,256,256]{2,1,0:T(8,128)(2,1)S(1)}, s32[8,128]{1,0:T(8,128)S(1)}) custom-call(s32[4]{0:T(128)S(1)} %copy-done.4, s32[2048]{0:T(1024)S(1)} %copy-done.2, s32[4]{0:T(128)S(1)} %copy-done.5, bf16[4,256,256]{2,1,0:T(8,128)(2,1)S(1)} %convolution_convert_fusion.1.spectra_ref), custom_call_target="tpu_custom_call" | custom-call | tf_op jit(solution)/shard_map/route/pallas_call | solution.py:362
  82.3 0.0 copy-start.6
  82.3 0.0 copy-start.7
  82.3 0.0 copy-done.1
  82.3 0.6 copy-done.6
  83.0 0.0 copy-done.7
  83.0 4.9 %refine.1 = (bf16[8,256,256]{2,1,0:T(8,128)(2,1)}, f32[8,8,128]{2,1,0:T(8,128)S(1)}) custom-call(s32[8,128]{1,0:T(8,128)S(1)} %get-tuple-element.6.label_ref, f32[64]{0:T(128)S(1)} %copy-done.6, f32[64]{0:T(128)S(1)} %copy-done.7, bf16[8,256,256]{2,1,0:T(8,128)(2,1)S(1)} %get-tuple-element.7.spectra_ref, bf16[8,256,256]{2,1,0:T(8,128)(2,1)S(1)} %copy-done.1), custom_call_target="tpu_custom_call" | custom-call | tf_op jit(solution)/shard_map/refine/pallas_call | solution.py:143
  87.9 0.0 copy-start.3
  87.9 0.6 copy-done.3
  88.5 21.6 %answer.1 = f32[8,128]{1,0:T(8,128)} custom-call(s32[4]{0:T(128)} %bin_ref.3, s32[2048]{0:T(1024)} %bin_place_ref.3, f32[8,8,128]{2,1,0:T(8,128)} %copy-done.3), custom_call_target="tpu_custom_call" | custom-call | tf_op jit(solution)/shard_map/answer/pallas_call | solution.py:418
  110.2 1.2 %slice_bitcast_fusion = f32[4]{0:T(128)} fusion(f32[8,128]{1,0:T(8,128)} %answer.1), kind=kLoop, calls=%fused_computation.42 | loop fusion | bytes 32 | tf_op jit(solution)/shard_map/squeeze | solution.py:438
Async XLA Ops:
  0.6 1.1 copy-start
  2.5 1.5 %copy-start.2 = (s32[2048]{0:T(1024)S(1)}, s32[2048]{0:T(1024)}, u32[]{:S(2)}) copy-start(s32[2048]{0:T(1024)} %bin_place_ref.3) | copy-start | bytes 24580
  2.5 1.5 %copy-start.4 = (s32[4]{0:T(128)S(1)}, s32[4]{0:T(128)}, u32[]{:S(2)}) copy-start(s32[4]{0:T(128)} %bin_ref.3) | copy-start | bytes 52
  2.6 1.5 %copy-start.5 = (s32[4]{0:T(128)S(1)}, s32[4]{0:T(128)}, u32[]{:S(2)}) copy-start(s32[4]{0:T(128)} %group_ref.1) | copy-start | bytes 52
  2.6 79.8 %copy-start.1 = (bf16[8,256,256]{2,1,0:T(8,128)(2,1)S(1)}, bf16[8,256,256]{2,1,0:T(8,128)(2,1)}, u32[]{:S(2)}) copy-start(bf16[8,256,256]{2,1,0:T(8,128)(2,1)} %refs_ref.1) | copy-start | bytes 3145732
  82.3 0.7 copy-start.6
  82.3 0.7 copy-start.7
  87.9 0.6 copy-start.3

commit v3 on v2

v3 whole, which is shorter than its diff:
```python
import math

import jax
import jax.numpy as jnp
from jax import lax
from jax.experimental import pallas as pl
from jax.experimental.pallas import tpu as pltpu
from jax.sharding import PartitionSpec as P

PRIOR_WEIGHT = 0.5
EPSILON = 1e-06
CONTRAST = 0.1
AMPLITUDE = math.sqrt(1.0 - CONTRAST * CONTRAST)
SIDE = 256
PIXELS = SIDE * SIDE
N_MIC, N_BIN, N_Z, N_Y = 8, 32, 8, 4
OWN, MINE = 8, 4
ROWS = 32
CTF_GROUPS = 64
DEPTHS = (64, 64, 64, 64)
CHUNKS = len(DEPTHS)
STARTS = [sum(DEPTHS[:c]) for c in range(CHUNKS)]
LAG = 2
MESH = pl.DeviceIdType.MESH


def hartley(side):
    k = lax.broadcasted_iota(jnp.int32, (side, side), 0)
    x = lax.broadcasted_iota(jnp.int32, (side, side), 1)
    angles = (k * x % side).astype(jnp.float32) * (2.0 * math.pi / side)
    return ((jnp.cos(angles) + jnp.sin(angles)) / math.sqrt(side)).astype(jnp.bfloat16)


def code_of(bin_ref, place_ref, group_ref, j):
    return place_ref[bin_ref[j]] * CTF_GROUPS + group_ref[j] + 1


def lanes_of(values):
    lane = lax.broadcasted_iota(jnp.int32, (8, 128), 1)
    tile = jnp.zeros((8, 128), jnp.int32)
    for j, value in enumerate(values):
        tile = jnp.where(lane == j, value, tile)
    return tile


def transform(offset_ref, basis_ref, images_ref, spectra):
    r = lax.broadcasted_iota(jnp.int32, (SIDE, SIDE), 0)
    c = lax.broadcasted_iota(jnp.int32, (SIDE, SIDE), 1)

    def one_hot(mask):
        return jnp.where(mask, 1.0, 0.0).astype(jnp.bfloat16)

    def dot(a, b):
        return jnp.dot(a, b, preferred_element_type=jnp.float32).astype(jnp.bfloat16)

    for j in range(MINE):
        moved = dot(one_hot(c == ((r + offset_ref[0, j]) & (SIDE - 1))), images_ref[j])
        moved = dot(moved, one_hot(r == ((c + offset_ref[1, j]) & (SIDE - 1))))
        spectra[j] = dot(dot(basis_ref[...], moved), basis_ref[...])


def kernel(bin_ref, bin_place_ref, group_ref, offset_ref, focus_ref, damp_ref, basis_ref, images_ref, refs_ref,
           out_ref, score_ref, *scratch):
    lines, packs = scratch[:CHUNKS], scratch[CHUNKS : 2 * CHUNKS]
    planes, parcels = scratch[2 * CHUNKS : 3 * CHUNKS], scratch[3 * CHUNKS : 4 * CHUNKS]
    (line_label, pack_label, plane_label, parcel_label, mine_label, line_code, plane_code, mine_code,
     z_send, z_recv, y_send, y_recv, m_send, m_recv, zl_send, zl_recv, yl_send, yl_recv,
     ml_send, ml_recv, am_send, am_recv, ay_send, ay_recv, az_send, az_recv, code_sem,
     spectra, owned, ctf, sums, total, row_scores, row, plane_scores, line_scores) = scratch[4 * CHUNKS :]
    mic, column = lax.axis_index("mic"), lax.axis_index("bin")
    z, y = column >> 2, column & (N_Y - 1)

    def at_z(d):
        return (mic, (((z + d) & (N_Z - 1)) << 2) + y)

    def at_y(d):
        return (mic, (z << 2) + ((y + d) & (N_Y - 1)))

    def at_mic(d):
        return ((mic + d) & (N_MIC - 1), column)

    def send(src, dst, send_sem, recv_sem, peer):
        copy = pltpu.make_async_remote_copy(
            src_ref=src, dst_ref=dst, send_sem=send_sem, recv_sem=recv_sem,
            device_id=peer, device_id_type=MESH,
        )
        copy.start()
        copies.append(copy)
        return copy

    copies = []
    peers = [at_z(d) for d in range(1, N_Z)] + [at_y(d) for d in range(1, N_Y)] + [at_mic(d) for d in range(1, N_MIC)]
    barrier = pltpu.get_barrier_semaphore()
    for peer in peers:
        pl.semaphore_signal(barrier, inc=1, device_id=peer, device_id_type=MESH)
    transform(offset_ref, basis_ref, images_ref, spectra)
    for block in range(2):
        total[block, N_MIC] = jnp.zeros((ROWS, SIDE), jnp.float32)
    sums[...] = jnp.zeros_like(sums)
    pl.semaphore_wait(barrier, len(peers))


    hops, y_copies, m_copies = {}, {}, {}
    pick_line, pick_plane = [], []
    half = N_Z // 2

    def hop(c, h):
        line = lines[c]
        if h == 1:
            line[0:MINE] = spectra[:, STARTS[c] : STARTS[c] + DEPTHS[c], :]
        for way in range(2):
            if h > 1:
                hops[c, way, h - 1].wait_recv()
            src = (1 - h) % N_Z if way == 0 else h - 1
            dst = N_Z - h if way == 0 else h
            low, count = 0, MINE
            if h == half:
                low, count = (MINE // 2) * way, MINE // 2
            hops[c, way, h] = send(
                line.at[pl.ds(src * MINE + low, count)], line.at[pl.ds(dst * MINE + low, count)],
                z_send.at[c, way, h - 1], z_recv.at[c, way, h - 1], at_z(1 if way == 0 else N_Z - 1),
            )

    def choose_line():
        for copy in line_labels:
            copy.wait_recv()
        fetch = pltpu.make_async_copy(line_label, line_code, code_sem.at[0])
        fetch.start()
        fetch.wait()
        keys = [[jnp.int32(0)] * MINE for _ in range(N_Y)]
        counts = [jnp.int32(0)] * N_Y
        for t in range(N_Z * MINE):
            code = line_code[t // MINE, 0, t % MINE]
            owner = (code - 1) >> 9
            here = ((owner >> 2) & (N_Z - 1)) == z
            away = (owner - y) & (N_Y - 1)
            key = code * (N_Z * MINE) + t
            for d in range(N_Y):
                hit = here & (away == d)
                rank = jnp.where(hit, counts[d], MINE)
                counts[d] = counts[d] + jnp.where(hit, 1, 0)
                keys[d] = [jnp.where(rank == k, key, keys[d][k]) for k in range(MINE)]
        pick_line.extend([[key & (N_Z * MINE - 1) for key in keys[d]] for d in range(N_Y)])
        for d in range(N_Y):
            tile = lanes_of([key >> 5 for key in keys[d]])
            if d == 0:
                plane_label[0] = tile
            else:
                pack_label[d - 1] = tile

    def to_plane(c):
        for way in range(2):
            hops[c, way, half].wait_recv()
        for d in range(N_Y):
            for k in range(MINE):
                tile = lines[c][pick_line[d][k]]
                if d == 0:
                    planes[c][k] = tile
                else:
                    packs[c][(d - 1) * MINE + k] = tile
        for d in range(1, N_Y):
            y_copies[c, d] = send(
                packs[c].at[pl.ds((d - 1) * MINE, MINE)], planes[c].at[pl.ds((N_Y - d) * MINE, MINE)],
                y_send.at[c, d - 1], y_recv.at[c, d - 1], at_y(d),
            )

    def choose_plane():
        fetch = pltpu.make_async_copy(plane_label, plane_code, code_sem.at[1])
        fetch.start()
        fetch.wait()
        keys = [jnp.int32(0)] * N_MIC
        for s in range(N_Y * MINE):
            code = plane_code[s // MINE, 0, s % MINE]
            away = (((code - 1) >> 14) - mic) & (N_MIC - 1)
            away = jnp.where(code > 0, away, N_MIC)
            key = code * (N_Y * MINE) + s
            keys = [jnp.where(away == d, key, keys[d]) for d in range(N_MIC)]
        pick_plane.extend([key & (N_Y * MINE - 1) for key in keys])
        for d in range(N_MIC):
            tile = jnp.full((8, 128), keys[d] >> 4, jnp.int32)
            if d == 0:
                mine_label[0] = tile
            else:
                parcel_label[d - 1] = tile

    def to_owner(c):
        for d in range(1, N_Y):
            y_copies[c, d].wait_recv()
        rows = pl.ds(STARTS[c], DEPTHS[c])
        for d in range(N_MIC):
            tile = planes[c][pick_plane[d]]
            if d == 0:
                owned[0, rows, :] = tile
            else:
                parcels[c][d - 1] = tile
        for d in range(1, N_MIC):
            m_copies[c, d] = send(
                parcels[c].at[d - 1], owned.at[N_MIC - d, rows, :],
                m_send.at[c, d - 1], m_recv.at[c, d - 1], at_mic(d),
            )

    line_label[0] = lanes_of([code_of(bin_ref, bin_place_ref, group_ref, j) for j in range(MINE)])
    line_labels = [
        send(line_label.at[0], line_label.at[N_Z - d], zl_send.at[d - 1], zl_recv.at[d - 1], at_z(d))
        for d in range(1, N_Z)
    ]
    def place_of(s):
        return ((mine_code[s, 0, 0] - 1) >> 6) & (OWN - 1)

    def tables():
        for copy in mine_labels:
            copy.wait_recv()
        fetch = pltpu.make_async_copy(mine_label, mine_code, code_sem.at[2])
        fetch.start()
        fetch.wait()
        slot = lax.broadcasted_iota(jnp.int32, (N_MIC, SIDE), 0)
        focus = jnp.zeros((N_MIC, SIDE), jnp.float32)
        damp = jnp.zeros((N_MIC, SIDE), jnp.float32)
        for s in range(N_MIC):
            group = (mine_code[s, 0, 0] - 1) & (CTF_GROUPS - 1)
            focus = jnp.where(slot == s, focus_ref[group], focus)
            damp = jnp.where(slot == s, damp_ref[group], damp)
        k = lax.broadcasted_iota(jnp.int32, (N_MIC, SIDE), 1)
        folded = jnp.minimum(k, SIDE - k).astype(jnp.float32) * (2.0 / SIDE)
        square = folded * folded
        sine, cosine = jnp.sin(focus * square), jnp.cos(focus * square)
        envelope = jnp.exp(-damp * square)
        row_sine = jnp.transpose(-sine * envelope)
        row_cosine = jnp.transpose(-cosine * envelope)
        col_sine = (AMPLITUDE * cosine - CONTRAST * sine) * envelope
        col_cosine = (AMPLITUDE * sine + CONTRAST * cosine) * envelope
        for s in range(N_MIC):
            ctf[s] = (
                row_sine[:, s : s + 1] * col_sine[s : s + 1, :]
                + row_cosine[:, s : s + 1] * col_cosine[s : s + 1, :]
            )

    def collect(start, depth, source, with_data):
        @pl.loop(0, N_MIC)
        def _(s):
            place = place_of(s)
            parts = [jnp.zeros((16, SIDE), jnp.float32)] * 3
            for low in range(start, start + depth, 16):
                rows = pl.ds(low, 16)
                predicted = ctf[s, rows, :] * source[place, rows, :].astype(jnp.float32)
                values = owned[s, rows, :].astype(jnp.float32)
                parts[0] = parts[0] + predicted * values
                parts[1] = parts[1] + predicted * predicted
                if with_data:
                    parts[2] = parts[2] + values * values
            for n in range(3 if with_data else 2):
                sums[s, n] += parts[n][:8] + parts[n][8:]

    def correlate():
        slot = lax.broadcasted_iota(jnp.int32, (N_MIC, 128), 0)
        means = []
        for n in range(3):
            mean = jnp.zeros((N_MIC, 128), jnp.float32)
            for s in range(N_MIC):
                mean = jnp.where(slot == s, jnp.sum(sums[s, n], keepdims=True), mean)
            means.append(mean / PIXELS)
        correlation = means[0] / jnp.sqrt((means[1] + EPSILON) * (means[2] + EPSILON))
        weight = 1.0 / (1.0 + jnp.exp(-SIDE * correlation))
        weight = weight.astype(jnp.bfloat16).astype(jnp.float32)
        weights = [jnp.where(mine_code[s, 0, 0] > 0, weight[s, 0], 0.0) for s in range(N_MIC)]
        return correlation, weights

    def update(weights, source, low, high):
        places = [place_of(s) for s in range(N_MIC)]
        before = []
        for s in range(N_MIC):
            index = jnp.int32(N_MIC)
            for other in range(s):
                index = jnp.where(places[other] == places[s], other, index)
            before.append(index)
        last = []
        for p in range(OWN):
            index = jnp.int32(N_MIC)
            for s in range(N_MIC):
                index = jnp.where(places[s] == p, s, index)
            last.append(index)

        @pl.loop(low, high)
        def _(i):
            rows = pl.ds(pl.multiple_of(i * ROWS, ROWS), ROWS)
            for s in range(N_MIC):
                table = ctf[s, rows, :]
                scaled = weights[s] * table
                term = (scaled * owned[s, rows, :].astype(jnp.float32)).astype(jnp.bfloat16).astype(jnp.float32)
                total[0, s] = term + total[0, before[s]]
                total[1, s] = scaled * table + total[1, before[s]]
            for p in range(OWN):
                top = total[0, last[p]] + PRIOR_WEIGHT * source[p, rows, :].astype(jnp.float32)
                out_ref[p, rows, :] = (top / (total[1, last[p]] + PRIOR_WEIGHT)).astype(jnp.bfloat16)

    plane_labels, mine_labels = [], []
    for step in range(1, CHUNKS + half + LAG + 2):
        if half < step <= half + CHUNKS:
            to_plane(step - half - 1)
        if half + LAG < step <= half + LAG + CHUNKS:
            to_owner(step - half - LAG - 1)
        for c in range(CHUNKS):
            if 1 <= step - c <= half:
                hop(c, step - c)
        if step == 3:
            choose_line()
            plane_labels += [
                send(pack_label.at[d - 1], plane_label.at[N_Y - d], yl_send.at[d - 1], yl_recv.at[d - 1], at_y(d))
                for d in range(1, N_Y)
            ]
        if step == 4:
            for copy in plane_labels:
                copy.wait_recv()
            choose_plane()
            mine_labels += [
                send(parcel_label.at[d - 1], mine_label.at[N_MIC - d], ml_send.at[d - 1], ml_recv.at[d - 1], at_mic(d))
                for d in range(1, N_MIC)
            ]
        if step == 6:
            tables()
        if half + LAG + 1 < step:
            c = step - half - LAG - 2
            for d in range(1, N_MIC):
                m_copies[c, d].wait_recv()
            collect(STARTS[c], DEPTHS[c], refs_ref, True)

    _, weights = correlate()
    update(weights, refs_ref, 0, SIDE // ROWS)
    for s in range(N_MIC):
        for n in range(2):
            sums[s, n] = jnp.zeros((8, SIDE), jnp.float32)
    collect(0, SIDE, out_ref, False)
    correlation, weights = correlate()

    for s in range(N_MIC):
        tile = jnp.broadcast_to(correlation[s : s + 1, :], (8, 128))
        if s == 0:
            row[0] = tile
        else:
            row_scores[s - 1] = tile
    by_mic = [
        send(row_scores.at[d - 1], row.at[N_MIC - d], am_send.at[d - 1], am_recv.at[d - 1], at_mic(d))
        for d in range(1, N_MIC)
    ]
    update(weights, out_ref, 0, SIDE // ROWS // 2)
    for copy in by_mic:
        copy.wait_recv()
    for d in range(N_MIC):
        plane_scores[0, pl.ds(d, 1), :] = row[d, 0:1, :]
    by_y = [
        send(plane_scores.at[0], plane_scores.at[N_Y - d], ay_send.at[d - 1], ay_recv.at[d - 1], at_y(d))
        for d in range(1, N_Y)
    ]
    update(weights, out_ref, SIDE // ROWS // 2, SIDE // ROWS)
    for copy in by_y:
        copy.wait_recv()
    line_scores[0] = plane_scores[...]
    by_z = [
        send(plane_scores, line_scores.at[N_Z - d], az_send.at[d - 1], az_recv.at[d - 1], at_z(d))
        for d in range(1, N_Z)
    ]
    for copy in by_z:
        copy.wait_recv()
    lane = lax.broadcasted_iota(jnp.int32, (8, 128), 1)
    scores = jnp.zeros((8, 128), jnp.float32)
    for j in range(MINE):
        owner = bin_place_ref[bin_ref[j]] >> 3
        away_z = ((owner >> 2) - z) & (N_Z - 1)
        away_y = (owner - y) & (N_Y - 1)
        away_mic = ((owner >> 5) - mic) & (N_MIC - 1)
        scores = jnp.where(lane == j, line_scores[away_z, away_y, pl.ds(away_mic, 1), :], scores)
    score_ref[...] = scores
    for copy in copies:
        copy.wait_send()


def body(images, offsets, ctf_group, particle_bin, bin_place, defocus, bfactor, references):
    smem = pl.BlockSpec(memory_space=pltpu.SMEM)
    vmem = pl.BlockSpec(memory_space=pltpu.VMEM)
    buffers = [pltpu.VMEM((n, depth, SIDE), jnp.bfloat16)
               for n in (N_Z * MINE, (N_Y - 1) * MINE, N_Y * MINE, N_MIC - 1) for depth in DEPTHS]
    labels = [pltpu.VMEM((n, 8, 128), jnp.int32) for n in (N_Z, N_Y - 1, N_Y, N_MIC - 1, N_MIC)]
    codes = [pltpu.SMEM((n, 8, 128), jnp.int32) for n in (N_Z, N_Y, N_MIC)]
    dma = pltpu.SemaphoreType.DMA
    sems = [dma(shape) for shape in ((CHUNKS, 2, N_Z // 2), (CHUNKS, N_Y - 1), (CHUNKS, N_MIC - 1),
                                     (N_Z - 1,), (N_Y - 1,), (N_MIC - 1,),
                                     (N_MIC - 1,), (N_Y - 1,), (N_Z - 1,)) for _ in range(2)]
    f32 = [pltpu.VMEM(shape, jnp.float32) for shape in (
        (N_MIC, SIDE, SIDE), (N_MIC, 3, 8, SIDE), (2, N_MIC + 1, ROWS, SIDE),
        (N_MIC - 1, 8, 128), (N_MIC, 8, 128), (N_Y, 8, 128), (N_Z, N_Y, 8, 128))]
    refined, scores = pl.pallas_call(
        kernel,
        out_shape=(
            jax.ShapeDtypeStruct((OWN, SIDE, SIDE), jnp.bfloat16),
            jax.ShapeDtypeStruct((8, 128), jnp.float32),
        ),
        in_specs=[smem] * 6 + [vmem] * 3,
        out_specs=(vmem, vmem),
        scratch_shapes=buffers + labels + codes + sems + [dma((3,))]
        + [pltpu.VMEM((MINE, SIDE, SIDE), jnp.bfloat16), pltpu.VMEM((N_MIC, SIDE, SIDE), jnp.bfloat16)] + f32,
        compiler_params=pltpu.CompilerParams(
            collective_id=0, has_side_effects=True, vmem_limit_bytes=32 << 20
        ),
        name="project",
    )(particle_bin, bin_place, ctf_group, offsets, defocus, bfactor, hartley(SIDE), images, references)
    return (refined, scores[0, :MINE])


def solution(mesh):
    tiles, items = P(("mic", "bin"), None, None), P(("mic", "bin"))
    return jax.shard_map(
        body,
        mesh=mesh,
        in_specs=(tiles, P(None, ("mic", "bin")), items, items, P(), P(), P(), tiles),
        out_specs=(tiles, items),
        check_vma=False,
    )
```

time: 112 us -> 88.4 us (0.79)
  Pallas kernels: 105 us -> 82.4 us
  matrix products: 2.28 us -> 0 us
    pallas_call x3 -> x1, Pallas kernels: 105 us -> 82.4 us  [body(): pl.pallas_call(kernel, out_shape=(jax.ShapeDtypeStruct((OWN, SIDE, SIDE),...]
    dot_general x2 -> x0, matrix products: 2.28 us -> none  [the longest x1 1.47 us: transform(): return dot('pky,ly->pkl', half, basis).astype(jnp.bfloat16)]
    unnamed x16 -> x17, local copies, waits for them, and re-layouts: 1.6 us -> 3.26 us
where the time goes in v3:
time: 88.4 us; the launch traced here: 88 us
  Pallas kernels  82.4 us (93%)
  local copies, waits for them, and re-layouts  3.77 us (4%)
  other arithmetic  1.1 us (1%)
    pallas_call x1, Pallas kernels, body(): pl.pallas_call(kernel, out_shape=(jax.ShapeDtypeStruct((OWN, SIDE, SIDE),...  82.4 us
    unnamed x17, local copies, waits for them, and re-layouts  3.26 us

profile of v3, /device:TPU:1, one launch (start us, length us, event | category | flops | bytes accessed | tf_op | source)
XLA Modules:
  0.0 88.0 jit_solution(9986289622356071283)
XLA Ops:
  0.6 0.0 copy-start.7
  0.6 0.0 copy-start.6
  0.7 0.0 copy-start.2
  0.7 0.0 copy-start.4
  0.7 0.0 copy-start.5
  0.7 0.0 copy-start.3
  0.7 1.1 %multiply_convert_fusion.basis_ref = bf16[256,256]{1,0:T(8,128)(2,1)S(1)} fusion(), kind=kLoop, calls=%fused_computation.6 | loop fusion | flops 1114112 | bytes 131072 | tf_op jit(solution)/shard_map/convert_element_type | solution.py:31
  1.8 0.0 copy-done.7
  1.8 0.0 copy-done.6
  1.8 0.0 copy-done.2
  1.8 0.0 copy-done.4
  1.8 0.0 copy-done.5
  1.9 0.0 copy-done.3
  1.9 0.0 copy-start
  1.9 1.2 %copy-done = bf16[8,256,256]{2,1,0:T(8,128)(2,1)S(1)} copy-done((bf16[8,256,256]{2,1,0:T(8,128)(2,1)S(1)}, bf16[8,256,256]{2,1,0:T(8,128)(2,1)}, u32[]{:S(2)}) %copy-start) | copy-done | bytes 1048600
  3.1 0.0 copy-start.1
  3.1 1.0 %copy-done.1 = bf16[4,256,256]{2,1,0:T(8,128)(2,1)S(1)} copy-done((bf16[4,256,256]{2,1,0:T(8,128)(2,1)S(1)}, bf16[4,256,256]{2,1,0:T(8,128)(2,1)}, u32[]{:S(2)}) %copy-start.1) | copy-done | bytes 524312
  4.1 82.4 %project.1 = (bf16[8,256,256]{2,1,0:T(8,128)(2,1)S(1)}, f32[8,128]{1,0:T(8,128)S(1)}) custom-call(s32[4]{0:T(128)S(1)} %copy-done.4, s32[2048]{0:T(1024)S(1)} %copy-done.2, s32[4]{0:T(128)S(1)} %copy-done.5, s32[2,4]{1,0:T(2,128)S(1)} %copy-done.3, f32[64]{0:T(128)S(1)} %copy-done.6, f32[64]{0:T(128)S(1)} %copy-done.7, ...), custom_call_target="tpu_custom_call" | custom-call | tf_op jit(solution)/shard_map/project/pallas_call | solution.py:391
  86.6 0.5 slice_bitcast_fusion
  87.1 1.0 %copy.11 = bf16[8,256,256]{2,1,0:T(8,128)(2,1)} copy(bf16[8,256,256]{2,1,0:T(8,128)(2,1)S(1)} %get-tuple-element.8) | data formatting | bytes 2097152
Async XLA Ops:
  0.6 1.2 %copy-start.7 = (f32[64]{0:T(128)S(1)}, f32[64]{0:T(128)}, u32[]{:S(2)}) copy-start(f32[64]{0:T(128)} %damp_ref.1) | copy-start | bytes 772
  0.6 1.2 %copy-start.6 = (f32[64]{0:T(128)S(1)}, f32[64]{0:T(128)}, u32[]{:S(2)}) copy-start(f32[64]{0:T(128)} %focus_ref.1) | copy-start | bytes 772
  0.7 1.2 %copy-start.2 = (s32[2048]{0:T(1024)S(1)}, s32[2048]{0:T(1024)}, u32[]{:S(2)}) copy-start(s32[2048]{0:T(1024)} %bin_place_ref.1) | copy-start | bytes 24580
  0.7 1.2 %copy-start.4 = (s32[4]{0:T(128)S(1)}, s32[4]{0:T(128)}, u32[]{:S(2)}) copy-start(s32[4]{0:T(128)} %bin_ref.1) | copy-start | bytes 52
  0.7 1.2 %copy-start.5 = (s32[4]{0:T(128)S(1)}, s32[4]{0:T(128)}, u32[]{:S(2)}) copy-start(s32[4]{0:T(128)} %group_ref.1) | copy-start | bytes 52
  0.7 1.2 %copy-start.3 = (s32[2,4]{1,0:T(2,128)S(1)}, s32[2,4]{1,0:T(2,128)}, u32[]{:S(2)}) copy-start(s32[2,4]{1,0:T(2,128)} %offset_ref.1) | copy-start | bytes 100
  1.9 1.2 %copy-start = (bf16[8,256,256]{2,1,0:T(8,128)(2,1)S(1)}, bf16[8,256,256]{2,1,0:T(8,128)(2,1)}, u32[]{:S(2)}) copy-start(bf16[8,256,256]{2,1,0:T(8,128)(2,1)} %refs_ref.1) | copy-start | bytes 3145732
  3.1 1.0 %copy-start.1 = (bf16[4,256,256]{2,1,0:T(8,128)(2,1)S(1)}, bf16[4,256,256]{2,1,0:T(8,128)(2,1)}, u32[]{:S(2)}) copy-start(bf16[4,256,256]{2,1,0:T(8,128)(2,1)} %images_ref.1) | copy-start | bytes 1572868

commit v4 on v3

--- a/solution.py
+++ b/solution.py
@@ -2,6 +2,8 @@
 
 import jax
 import jax.numpy as jnp
+import ml_dtypes
+import numpy as np
 from jax import lax
 from jax.experimental import pallas as pl
 from jax.experimental.pallas import tpu as pltpu
@@ -17,18 +19,25 @@
 OWN, MINE = 8, 4
 ROWS = 32
 CTF_GROUPS = 64
-DEPTHS = (64, 64, 64, 64)
+DEPTHS = (64, 64, 64, 32, 32)
 CHUNKS = len(DEPTHS)
 STARTS = [sum(DEPTHS[:c]) for c in range(CHUNKS)]
-LAG = 2
+HOP, PLANE, OWNER = 0, 1, 2
+ORDER = (
+    (HOP, 2, 1), (HOP, 0, 1), (HOP, 1, 1), (HOP, 0, 2), (HOP, 1, 2), (HOP, 0, 3),
+    (HOP, 1, 3), (HOP, 0, 4), (HOP, 2, 2), (HOP, 1, 4), (PLANE, 0, 0), (HOP, 3, 1),
+    (HOP, 2, 3), (PLANE, 1, 0), (HOP, 4, 1), (HOP, 3, 2), (HOP, 2, 4), (HOP, 4, 2),
+    (HOP, 3, 3), (PLANE, 2, 0), (HOP, 4, 3), (HOP, 3, 4), (OWNER, 1, 0), (HOP, 4, 4),
+    (PLANE, 3, 0), (OWNER, 0, 0), (PLANE, 4, 0), (OWNER, 2, 0), (OWNER, 3, 0), (OWNER, 4, 0),
+)
+LABELS_AT = 10
 MESH = pl.DeviceIdType.MESH
 
 
-def hartley(side):
-    k = lax.broadcasted_iota(jnp.int32, (side, side), 0)
-    x = lax.broadcasted_iota(jnp.int32, (side, side), 1)
-    angles = (k * x % side).astype(jnp.float32) * (2.0 * math.pi / side)
-    return ((jnp.cos(angles) + jnp.sin(angles)) / math.sqrt(side)).astype(jnp.bfloat16)
+def hartley():
+    k = np.arange(SIDE)
+    angles = (np.outer(k, k) % SIDE).astype(np.float32) * np.float32(2.0 * math.pi / SIDE)
+    return ((np.cos(angles) + np.sin(angles)) / np.float32(math.sqrt(SIDE))).astype(ml_dtypes.bfloat16)
 
 
 def code_of(bin_ref, place_ref, group_ref, j):
@@ -59,14 +68,15 @@
         spectra[j] = dot(dot(basis_ref[...], moved), basis_ref[...])
 
 
-def kernel(bin_ref, bin_place_ref, group_ref, offset_ref, focus_ref, damp_ref, basis_ref, images_ref, refs_ref,
-           out_ref, score_ref, *scratch):
+def kernel(*refs):
+    inputs, (out_ref, score_ref), scratch = refs[:9], refs[9:11], refs[20:]
+    bin_ref, bin_place_ref, group_ref, offset_ref, focus_ref, damp_ref, basis_ref, images_ref, refs_ref = held = refs[11:20]
     lines, packs = scratch[:CHUNKS], scratch[CHUNKS : 2 * CHUNKS]
     planes, parcels = scratch[2 * CHUNKS : 3 * CHUNKS], scratch[3 * CHUNKS : 4 * CHUNKS]
     (line_label, pack_label, plane_label, parcel_label, mine_label, line_code, plane_code, mine_code,
      z_send, z_recv, y_send, y_recv, m_send, m_recv, zl_send, zl_recv, yl_send, yl_recv,
      ml_send, ml_recv, am_send, am_recv, ay_send, ay_recv, az_send, az_recv, code_sem,
-     spectra, owned, ctf, sums, total, row_scores, row, plane_scores, line_scores) = scratch[4 * CHUNKS :]
+     load_sem, spectra, owned, ctf, sums, total, row_scores, row, plane_scores, line_scores) = scratch[4 * CHUNKS :]
     mic, column = lax.axis_index("mic"), lax.axis_index("bin")
     z, y = column >> 2, column & (N_Y - 1)
 
@@ -89,10 +99,18 @@
         return copy
 
     copies = []
+    loads = [
+        pltpu.make_async_copy(src, dst, load_sem.at[n])
+        for n, (src, dst) in enumerate(zip(inputs, held))
+    ]
+    for load in loads:
+        load.start()
     peers = [at_z(d) for d in range(1, N_Z)] + [at_y(d) for d in range(1, N_Y)] + [at_mic(d) for d in range(1, N_MIC)]
     barrier = pltpu.get_barrier_semaphore()
     for peer in peers:
         pl.semaphore_signal(barrier, inc=1, device_id=peer, device_id_type=MESH)
+    for load in loads[:8]:
+        load.wait()
     transform(offset_ref, basis_ref, images_ref, spectra)
     for block in range(2):
         total[block, N_MIC] = jnp.zeros((ROWS, SIDE), jnp.float32)
@@ -207,7 +225,7 @@
     def place_of(s):
         return ((mine_code[s, 0, 0] - 1) >> 6) & (OWN - 1)
 
-    def tables():
+    def tables(mine_labels):
         for copy in mine_labels:
             copy.wait_recv()
         fetch = pltpu.make_async_copy(mine_label, mine_code, code_sem.at[2])
@@ -293,36 +311,36 @@
                 top = total[0, last[p]] + PRIOR_WEIGHT * source[p, rows, :].astype(jnp.float32)
                 out_ref[p, rows, :] = (top / (total[1, last[p]] + PRIOR_WEIGHT)).astype(jnp.bfloat16)
 
-    plane_labels, mine_labels = [], []
-    for step in range(1, CHUNKS + half + LAG + 2):
-        if half < step <= half + CHUNKS:
-            to_plane(step - half - 1)
-        if half + LAG < step <= half + LAG + CHUNKS:
-            to_owner(step - half - LAG - 1)
-        for c in range(CHUNKS):
-            if 1 <= step - c <= half:
-                hop(c, step - c)
-        if step == 3:
+    owners_done = []
+    for n, (kind, c, h) in enumerate(ORDER):
+        if n == LABELS_AT:
             choose_line()
-            plane_labels += [
+            plane_labels = [
                 send(pack_label.at[d - 1], plane_label.at[N_Y - d], yl_send.at[d - 1], yl_recv.at[d - 1], at_y(d))
                 for d in range(1, N_Y)
             ]
-        if step == 4:
-            for copy in plane_labels:
-                copy.wait_recv()
-            choose_plane()
-            mine_labels += [
-                send(parcel_label.at[d - 1], mine_label.at[N_MIC - d], ml_send.at[d - 1], ml_recv.at[d - 1], at_mic(d))
-                for d in range(1, N_MIC)
-            ]
-        if step == 6:
-            tables()
-        if half + LAG + 1 < step:
-            c = step - half - LAG - 2
-            for d in range(1, N_MIC):
-                m_copies[c, d].wait_recv()
-            collect(STARTS[c], DEPTHS[c], refs_ref, True)
+        if kind == HOP:
+            hop(c, h)
+        elif kind == PLANE:
+            to_plane(c)
+        else:
+            if not owners_done:
+                for copy in plane_labels:
+                    copy.wait_recv()
+                choose_plane()
+                mine_labels = [
+                    send(parcel_label.at[d - 1], mine_label.at[N_MIC - d], ml_send.at[d - 1], ml_recv.at[d - 1], at_mic(d))
+                    for d in range(1, N_MIC)
+                ]
+            to_owner(c)
+            owners_done.append(c)
+            if len(owners_done) == CHUNKS - 1:
+                tables(mine_labels)
+    loads[8].wait()
+    for c in owners_done:
+        for d in range(1, N_MIC):
+            m_copies[c, d].wait_recv()
+        collect(STARTS[c], DEPTHS[c], refs_ref, True)
 
     _, weights = correlate()
     update(weights, refs_ref, 0, SIDE // ROWS)
@@ -375,7 +393,8 @@
 
 
 def body(images, offsets, ctf_group, particle_bin, bin_place, defocus, bfactor, references):
-    smem = pl.BlockSpec(memory_space=pltpu.SMEM)
+    inputs = (particle_bin, bin_place, ctf_group, offsets, defocus, bfactor, jnp.asarray(hartley()), images, references)
+    held = [(pltpu.SMEM if n < 6 else pltpu.VMEM)(x.shape, x.dtype) for n, x in enumerate(inputs)]
     vmem = pl.BlockSpec(memory_space=pltpu.VMEM)
     buffers = [pltpu.VMEM((n, depth, SIDE), jnp.bfloat16)
                for n in (N_Z * MINE, (N_Y - 1) * MINE, N_Y * MINE, N_MIC - 1) for depth in DEPTHS]
@@ -394,15 +413,16 @@
             jax.ShapeDtypeStruct((OWN, SIDE, SIDE), jnp.bfloat16),
             jax.ShapeDtypeStruct((8, 128), jnp.float32),
         ),
-        in_specs=[smem] * 6 + [vmem] * 3,
+        in_specs=[pl.BlockSpec(memory_space=pltpu.HBM)] * 9,
         out_specs=(vmem, vmem),
-        scratch_shapes=buffers + labels + codes + sems + [dma((3,))]
+        scratch_shapes=held + buffers + labels + codes + sems + [dma((3,))]
++ [dma((9,))]
         + [pltpu.VMEM((MINE, SIDE, SIDE), jnp.bfloat16), pltpu.VMEM((N_MIC, SIDE, SIDE), jnp.bfloat16)] + f32,
         compiler_params=pltpu.CompilerParams(
             collective_id=0, has_side_effects=True, vmem_limit_bytes=32 << 20
         ),
         name="project",
-    )(particle_bin, bin_place, ctf_group, offsets, defocus, bfactor, hartley(SIDE), images, references)
+    )(*[pltpu.with_memory_space_constraint(x, pltpu.HBM) for x in inputs])
     return (refined, scores[0, :MINE])
 
 

time: 88.4 us -> 82 us (0.928)
  Pallas kernels: 82.4 us -> 79.3 us
  local copies, waits for them, and re-layouts: 3.77 us -> 1.48 us
  other arithmetic: 1.1 us -> 0 us
    pallas_call x1, Pallas kernels: 82.4 us -> 79.3 us  [body(): pl.pallas_call(kernel, out_shape=(jax.ShapeDtypeStruct((OWN, SIDE, SIDE),...]
    unnamed x17 -> x1, local copies, waits for them, and re-layouts: 3.26 us -> 0.97 us
    convert_element_type x1 -> x0, other arithmetic: 1.1 us -> none  [hartley(): ((jnp.cos(angles) + jnp.sin(angles)) / math.sqrt(side)).astype(jnp.bfloat16)]
where the time goes in v4:
time: 82 us; the launch traced here: 81.5 us
  Pallas kernels  79.3 us (97%)
  local copies, waits for them, and re-layouts  1.48 us (2%)
    pallas_call x1, Pallas kernels, body(): pl.pallas_call(kernel, out_shape=(jax.ShapeDtypeStruct((OWN, SIDE, SIDE),...  79.3 us

profile of v4, /device:TPU:1, one launch (start us, length us, event | category | flops | bytes accessed | tf_op | source)
XLA Modules:
  0.0 81.5 jit_solution(2389796401596043433)
XLA Ops:
  0.6 79.3 %project.1 = (bf16[8,256,256]{2,1,0:T(8,128)(2,1)S(1)}, f32[8,128]{1,0:T(8,128)S(1)}) custom-call(s32[4]{0:T(128)} %refs_0_.1, s32[2048]{0:T(1024)} %refs_1_.1, s32[4]{0:T(128)} %refs_2_.1, s32[2,4]{1,0:T(2,128)} %refs_3_.1, f32[64]{0:T(128)} %refs_4_.1, f32[64]{0:T(128)} %refs_5_.1, bf16[256,256]{1,0:T(8,128)(2,1)} %constant.2.clone.refs_6_, ...), custom_call_target="tpu_custom_call" | custom-call | tf_op jit(solution)/shard_map/project/pallas_call | solution.py:410
  80.0 0.5 slice_bitcast_fusion
  80.5 1.0 %copy.12 = bf16[8,256,256]{2,1,0:T(8,128)(2,1)} copy(bf16[8,256,256]{2,1,0:T(8,128)(2,1)S(1)} %get-tuple-element.8) | data formatting | bytes 2097152

commit v5 on v4

--- a/solution.py
+++ b/solution.py
@@ -30,7 +30,7 @@
     (HOP, 3, 3), (PLANE, 2, 0), (HOP, 4, 3), (HOP, 3, 4), (OWNER, 1, 0), (HOP, 4, 4),
     (PLANE, 3, 0), (OWNER, 0, 0), (PLANE, 4, 0), (OWNER, 2, 0), (OWNER, 3, 0), (OWNER, 4, 0),
 )
-LABELS_AT = 10
+LABELS_AT = (6, 7, 11, 12, 16, 19)
 MESH = pl.DeviceIdType.MESH
 
 
@@ -140,11 +140,6 @@
             )
 
     def choose_line():
-        for copy in line_labels:
-            copy.wait_recv()
-        fetch = pltpu.make_async_copy(line_label, line_code, code_sem.at[0])
-        fetch.start()
-        fetch.wait()
         keys = [[jnp.int32(0)] * MINE for _ in range(N_Y)]
         counts = [jnp.int32(0)] * N_Y
         for t in range(N_Z * MINE):
@@ -183,9 +178,6 @@
             )
 
     def choose_plane():
-        fetch = pltpu.make_async_copy(plane_label, plane_code, code_sem.at[1])
-        fetch.start()
-        fetch.wait()
         keys = [jnp.int32(0)] * N_MIC
         for s in range(N_Y * MINE):
             code = plane_code[s // MINE, 0, s % MINE]
@@ -217,125 +209,129 @@
                 m_send.at[c, d - 1], m_recv.at[c, d - 1], at_mic(d),
             )
 
-    line_label[0] = lanes_of([code_of(bin_ref, bin_place_ref, group_ref, j) for j in range(MINE)])
-    line_labels = [
-        send(line_label.at[0], line_label.at[N_Z - d], zl_send.at[d - 1], zl_recv.at[d - 1], at_z(d))
-        for d in range(1, N_Z)
-    ]
-    def place_of(s):
-        return ((mine_code[s, 0, 0] - 1) >> 6) & (OWN - 1)
-
-    def tables(mine_labels):
-        for copy in mine_labels:
+    def read_codes(labels, label, code, n):
+        for copy in labels:
             copy.wait_recv()
-        fetch = pltpu.make_async_copy(mine_label, mine_code, code_sem.at[2])
+        fetch = pltpu.make_async_copy(label.at[:, 0:1], code.at[:, 0:1], code_sem.at[n])
         fetch.start()
-        fetch.wait()
-        slot = lax.broadcasted_iota(jnp.int32, (N_MIC, SIDE), 0)
-        focus = jnp.zeros((N_MIC, SIDE), jnp.float32)
-        damp = jnp.zeros((N_MIC, SIDE), jnp.float32)
-        for s in range(N_MIC):
-            group = (mine_code[s, 0, 0] - 1) & (CTF_GROUPS - 1)
-            focus = jnp.where(slot == s, focus_ref[group], focus)
-            damp = jnp.where(slot == s, damp_ref[group], damp)
-        k = lax.broadcasted_iota(jnp.int32, (N_MIC, SIDE), 1)
-        folded = jnp.minimum(k, SIDE - k).astype(jnp.float32) * (2.0 / SIDE)
-        square = folded * folded
-        sine, cosine = jnp.sin(focus * square), jnp.cos(focus * square)
-        envelope = jnp.exp(-damp * square)
-        row_sine = jnp.transpose(-sine * envelope)
-        row_cosine = jnp.transpose(-cosine * envelope)
-        col_sine = (AMPLITUDE * cosine - CONTRAST * sine) * envelope
-        col_cosine = (AMPLITUDE * sine + CONTRAST * cosine) * envelope
-        for s in range(N_MIC):
-            ctf[s] = (
-                row_sine[:, s : s + 1] * col_sine[s : s + 1, :]
-                + row_cosine[:, s : s + 1] * col_cosine[s : s + 1, :]
-            )
-
-    def collect(start, depth, source, with_data):
-        @pl.loop(0, N_MIC)
-        def _(s):
-            place = place_of(s)
-            parts = [jnp.zeros((16, SIDE), jnp.float32)] * 3
-            for low in range(start, start + depth, 16):
-                rows = pl.ds(low, 16)
-                predicted = ctf[s, rows, :] * source[place, rows, :].astype(jnp.float32)
-                values = owned[s, rows, :].astype(jnp.float32)
-                parts[0] = parts[0] + predicted * values
-                parts[1] = parts[1] + predicted * predicted
-                if with_data:
-                    parts[2] = parts[2] + values * values
-            for n in range(3 if with_data else 2):
-                sums[s, n] += parts[n][:8] + parts[n][8:]
-
-    def correlate():
-        slot = lax.broadcasted_iota(jnp.int32, (N_MIC, 128), 0)
-        means = []
-        for n in range(3):
-            mean = jnp.zeros((N_MIC, 128), jnp.float32)
-            for s in range(N_MIC):
-                mean = jnp.where(slot == s, jnp.sum(sums[s, n], keepdims=True), mean)
-            means.append(mean / PIXELS)
-        correlation = means[0] / jnp.sqrt((means[1] + EPSILON) * (means[2] + EPSILON))
-        weight = 1.0 / (1.0 + jnp.exp(-SIDE * correlation))
-        weight = weight.astype(jnp.bfloat16).astype(jnp.float32)
-        weights = [jnp.where(mine_code[s, 0, 0] > 0, weight[s, 0], 0.0) for s in range(N_MIC)]
-        return correlation, weights
-
-    def update(weights, source, low, high):
-        places = [place_of(s) for s in range(N_MIC)]
-        before = []
-        for s in range(N_MIC):
-            index = jnp.int32(N_MIC)
-            for other in range(s):
-                index = jnp.where(places[other] == places[s], other, index)
-            before.append(index)
-        last = []
-        for p in range(OWN):
-            index = jnp.int32(N_MIC)
-            for s in range(N_MIC):
-                index = jnp.where(places[s] == p, s, index)
-            last.append(index)
-
-        @pl.loop(low, high)
-        def _(i):
-            rows = pl.ds(pl.multiple_of(i * ROWS, ROWS), ROWS)
-            for s in range(N_MIC):
-                table = ctf[s, rows, :]
-                scaled = weights[s] * table
-                term = (scaled * owned[s, rows, :].astype(jnp.float32)).astype(jnp.bfloat16).astype(jnp.float32)
-                total[0, s] = term + total[0, before[s]]
-                total[1, s] = scaled * table + total[1, before[s]]
-            for p in range(OWN):
-                top = total[0, last[p]] + PRIOR_WEIGHT * source[p, rows, :].astype(jnp.float32)
-                out_ref[p, rows, :] = (top / (total[1, last[p]] + PRIOR_WEIGHT)).astype(jnp.bfloat16)
+        return fetch
 
     owners_done = []
     for n, (kind, c, h) in enumerate(ORDER):
-        if n == LABELS_AT:
+        if n == 3:
+            line_label[0] = lanes_of([code_of(bin_ref, bin_place_ref, group_ref, j) for j in range(MINE)])
+            line_labels = [
+                send(line_label.at[0, 0:1], line_label.at[N_Z - d, 0:1], zl_send.at[d - 1], zl_recv.at[d - 1], at_z(d))
+                for d in range(1, N_Z)
+            ]
+            def place_of(s):
+                return ((mine_code[s, 0, 0] - 1) >> 6) & (OWN - 1)
+            def tables():
+                slot = lax.broadcasted_iota(jnp.int32, (N_MIC, SIDE), 0)
+                focus = jnp.zeros((N_MIC, SIDE), jnp.float32)
+                damp = jnp.zeros((N_MIC, SIDE), jnp.float32)
+                for s in range(N_MIC):
+                    group = (mine_code[s, 0, 0] - 1) & (CTF_GROUPS - 1)
+                    focus = jnp.where(slot == s, focus_ref[group], focus)
+                    damp = jnp.where(slot == s, damp_ref[group], damp)
+                k = lax.broadcasted_iota(jnp.int32, (N_MIC, SIDE), 1)
+                folded = jnp.minimum(k, SIDE - k).astype(jnp.float32) * (2.0 / SIDE)
+                square = folded * folded
+                sine, cosine = jnp.sin(focus * square), jnp.cos(focus * square)
+                envelope = jnp.exp(-damp * square)
+                row_sine = jnp.transpose(-sine * envelope)
+                row_cosine = jnp.transpose(-cosine * envelope)
+                col_sine = (AMPLITUDE * cosine - CONTRAST * sine) * envelope
+                col_cosine = (AMPLITUDE * sine + CONTRAST * cosine) * envelope
+                for s in range(N_MIC):
+                    ctf[s] = (
+                        row_sine[:, s : s + 1] * col_sine[s : s + 1, :]
+                        + row_cosine[:, s : s + 1] * col_cosine[s : s + 1, :]
+                    )
+            def collect(start, depth, source, with_data):
+                @pl.loop(0, N_MIC)
+                def _(s):
+                    place = place_of(s)
+                    parts = [jnp.zeros((16, SIDE), jnp.float32)] * 3
+                    for low in range(start, start + depth, 16):
+                        rows = pl.ds(low, 16)
+                        predicted = ctf[s, rows, :] * source[place, rows, :].astype(jnp.float32)
+                        values = owned[s, rows, :].astype(jnp.float32)
+                        parts[0] = parts[0] + predicted * values
+                        parts[1] = parts[1] + predicted * predicted
+                        if with_data:
+                            parts[2] = parts[2] + values * values
+                    for n in range(3 if with_data else 2):
+                        sums[s, n] += parts[n][:8] + parts[n][8:]
+            def correlate():
+                slot = lax.broadcasted_iota(jnp.int32, (N_MIC, 128), 0)
+                means = []
+                for n in range(3):
+                    mean = jnp.zeros((N_MIC, 128), jnp.float32)
+                    for s in range(N_MIC):
+                        mean = jnp.where(slot == s, jnp.sum(sums[s, n], keepdims=True), mean)
+                    means.append(mean / PIXELS)
+                correlation = means[0] / jnp.sqrt((means[1] + EPSILON) * (means[2] + EPSILON))
+                weight = 1.0 / (1.0 + jnp.exp(-SIDE * correlation))
+                weight = weight.astype(jnp.bfloat16).astype(jnp.float32)
+                weights = [jnp.where(mine_code[s, 0, 0] > 0, weight[s, 0], 0.0) for s in range(N_MIC)]
+                return correlation, weights
+            def update(weights, source, low, high):
+                places = [place_of(s) for s in range(N_MIC)]
+                before = []
+                for s in range(N_MIC):
+                    index = jnp.int32(N_MIC)
+                    for other in range(s):
+                        index = jnp.where(places[other] == places[s], other, index)
+                    before.append(index)
+                last = []
+                for p in range(OWN):
+                    index = jnp.int32(N_MIC)
+                    for s in range(N_MIC):
+                        index = jnp.where(places[s] == p, s, index)
+                    last.append(index)
+                @pl.loop(low, high)
+                def _(i):
+                    rows = pl.ds(pl.multiple_of(i * ROWS, ROWS), ROWS)
+                    for s in range(N_MIC):
+                        table = ctf[s, rows, :]
+                        scaled = weights[s] * table
+                        term = (scaled * owned[s, rows, :].astype(jnp.float32)).astype(jnp.bfloat16).astype(jnp.float32)
+                        total[0, s] = term + total[0, before[s]]
+                        total[1, s] = scaled * table + total[1, before[s]]
+                    for p in range(OWN):
+                        top = total[0, last[p]] + PRIOR_WEIGHT * source[p, rows, :].astype(jnp.float32)
+                        out_ref[p, rows, :] = (top / (total[1, last[p]] + PRIOR_WEIGHT)).astype(jnp.bfloat16)
+        if n == LABELS_AT[0]:
+            fetch = read_codes(line_labels, line_label, line_code, 0)
+        if n == LABELS_AT[1]:
+            fetch.wait()
             choose_line()
             plane_labels = [
-                send(pack_label.at[d - 1], plane_label.at[N_Y - d], yl_send.at[d - 1], yl_recv.at[d - 1], at_y(d))
+                send(pack_label.at[d - 1, 0:1], plane_label.at[N_Y - d, 0:1], yl_send.at[d - 1], yl_recv.at[d - 1], at_y(d))
                 for d in range(1, N_Y)
             ]
+        if n == LABELS_AT[2]:
+            fetch = read_codes(plane_labels, plane_label, plane_code, 1)
+        if n == LABELS_AT[3]:
+            fetch.wait()
+            choose_plane()
+            mine_labels = [
+                send(parcel_label.at[d - 1, 0:1], mine_label.at[N_MIC - d, 0:1], ml_send.at[d - 1], ml_recv.at[d - 1], at_mic(d))
+                for d in range(1, N_MIC)
+            ]
+        if n == LABELS_AT[4]:
+            fetch = read_codes(mine_labels, mine_label, mine_code, 2)
+        if n == LABELS_AT[5]:
+            fetch.wait()
+            tables()
         if kind == HOP:
             hop(c, h)
         elif kind == PLANE:
             to_plane(c)
         else:
-            if not owners_done:
-                for copy in plane_labels:
-                    copy.wait_recv()
-                choose_plane()
-                mine_labels = [
-                    send(parcel_label.at[d - 1], mine_label.at[N_MIC - d], ml_send.at[d - 1], ml_recv.at[d - 1], at_mic(d))
-                    for d in range(1, N_MIC)
-                ]
             to_owner(c)
             owners_done.append(c)
-            if len(owners_done) == CHUNKS - 1:
-                tables(mine_labels)
     loads[8].wait()
     for c in owners_done:
         for d in range(1, N_MIC):
@@ -344,29 +340,29 @@
 
     _, weights = correlate()
     update(weights, refs_ref, 0, SIDE // ROWS)
+    routed = len(copies)
     for s in range(N_MIC):
         for n in range(2):
             sums[s, n] = jnp.zeros((8, SIDE), jnp.float32)
     collect(0, SIDE, out_ref, False)
     correlation, weights = correlate()
 
-    for s in range(N_MIC):
-        tile = jnp.broadcast_to(correlation[s : s + 1, :], (8, 128))
-        if s == 0:
-            row[0] = tile
-        else:
-            row_scores[s - 1] = tile
+    row_scores[...] = correlation
+    row[0:1, :] = correlation[0:1, :]
     by_mic = [
-        send(row_scores.at[d - 1], row.at[N_MIC - d], am_send.at[d - 1], am_recv.at[d - 1], at_mic(d))
+        send(row_scores.at[d : d + 1], row.at[N_MIC - d : N_MIC - d + 1], am_send.at[d - 1], am_recv.at[d - 1], at_mic(d))
         for d in range(1, N_MIC)
     ]
     update(weights, out_ref, 0, SIDE // ROWS // 2)
+    for copy in copies[:routed]:
+        copy.wait_send()
     for copy in by_mic:
         copy.wait_recv()
-    for d in range(N_MIC):
-        plane_scores[0, pl.ds(d, 1), :] = row[d, 0:1, :]
+    lane = lax.broadcasted_iota(jnp.int32, (8, 128), 1)
+    of_mic = lax.broadcasted_iota(jnp.int32, (8, 128), 0)
+    plane_scores[0:1, :] = jnp.sum(jnp.where(lane == of_mic, row[...], 0.0), axis=0, keepdims=True)
     by_y = [
-        send(plane_scores.at[0], plane_scores.at[N_Y - d], ay_send.at[d - 1], ay_recv.at[d - 1], at_y(d))
+        send(plane_scores.at[0:1], plane_scores.at[N_Y - d : N_Y - d + 1], ay_send.at[d - 1], ay_recv.at[d - 1], at_y(d))
         for d in range(1, N_Y)
     ]
     update(weights, out_ref, SIDE // ROWS // 2, SIDE // ROWS)
@@ -379,16 +375,16 @@
     ]
     for copy in by_z:
         copy.wait_recv()
-    lane = lax.broadcasted_iota(jnp.int32, (8, 128), 1)
     scores = jnp.zeros((8, 128), jnp.float32)
     for j in range(MINE):
         owner = bin_place_ref[bin_ref[j]] >> 3
         away_z = ((owner >> 2) - z) & (N_Z - 1)
         away_y = (owner - y) & (N_Y - 1)
         away_mic = ((owner >> 5) - mic) & (N_MIC - 1)
-        scores = jnp.where(lane == j, line_scores[away_z, away_y, pl.ds(away_mic, 1), :], scores)
+        found = jnp.where(lane[0:1, :] == away_mic, line_scores[away_z, pl.ds(away_y, 1), :], 0.0)
+        scores = jnp.where(lane == j, jnp.sum(found, keepdims=True), scores)
     score_ref[...] = scores
-    for copy in copies:
+    for copy in copies[routed:]:
         copy.wait_send()
 
 
@@ -406,7 +402,7 @@
                                      (N_MIC - 1,), (N_Y - 1,), (N_Z - 1,)) for _ in range(2)]
     f32 = [pltpu.VMEM(shape, jnp.float32) for shape in (
         (N_MIC, SIDE, SIDE), (N_MIC, 3, 8, SIDE), (2, N_MIC + 1, ROWS, SIDE),
-        (N_MIC - 1, 8, 128), (N_MIC, 8, 128), (N_Y, 8, 128), (N_Z, N_Y, 8, 128))]
+        (N_MIC, 128), (N_MIC, 128), (N_Y, 128), (N_Z, N_Y, 128))]
     refined, scores = pl.pallas_call(
         kernel,
         out_shape=(

time: 82 us -> 79.3 us (0.967)
  Pallas kernels: 79.3 us -> 76.9 us
    pallas_call x1, Pallas kernels: 79.3 us -> 76.9 us  [body(): pl.pallas_call(kernel, out_shape=(jax.ShapeDtypeStruct((OWN, SIDE, SIDE),...]
where the time goes in v5:
time: 79.3 us; the launch traced here: 79 us
  Pallas kernels  76.9 us (97%)
  local copies, waits for them, and re-layouts  1.48 us (2%)
    pallas_call x1, Pallas kernels, body(): pl.pallas_call(kernel, out_shape=(jax.ShapeDtypeStruct((OWN, SIDE, SIDE),...  76.9 us

profile of v5, /device:TPU:1, one launch (start us, length us, event | category | flops | bytes accessed | tf_op | source)
XLA Modules:
  0.0 79.0 jit_solution(7989016815552412410)
XLA Ops:
  0.6 76.9 %project.1 = (bf16[8,256,256]{2,1,0:T(8,128)(2,1)S(1)}, f32[8,128]{1,0:T(8,128)S(1)}) custom-call(s32[4]{0:T(128)} %refs_0_.1, s32[2048]{0:T(1024)} %refs_1_.1, s32[4]{0:T(128)} %refs_2_.1, s32[2,4]{1,0:T(2,128)} %refs_3_.1, f32[64]{0:T(128)} %refs_4_.1, f32[64]{0:T(128)} %refs_5_.1, bf16[256,256]{1,0:T(8,128)(2,1)} %constant.2.clone.refs_6_, ...), custom_call_target="tpu_custom_call" | custom-call | tf_op jit(solution)/shard_map/project/pallas_call | solution.py:406
  77.5 0.5 slice_bitcast_fusion
  78.0 1.0 %copy.12 = bf16[8,256,256]{2,1,0:T(8,128)(2,1)} copy(bf16[8,256,256]{2,1,0:T(8,128)(2,1)S(1)} %get-tuple-element.8) | data formatting | bytes 2097152

commit v6 on v4

--- a/solution.py
+++ b/solution.py
@@ -24,13 +24,13 @@
 STARTS = [sum(DEPTHS[:c]) for c in range(CHUNKS)]
 HOP, PLANE, OWNER = 0, 1, 2
 ORDER = (
-    (HOP, 2, 1), (HOP, 0, 1), (HOP, 1, 1), (HOP, 0, 2), (HOP, 1, 2), (HOP, 0, 3),
+    (HOP, 0, 1), (HOP, 1, 1), (HOP, 0, 2), (HOP, 1, 2), (HOP, 0, 3), (HOP, 2, 1),
     (HOP, 1, 3), (HOP, 0, 4), (HOP, 2, 2), (HOP, 1, 4), (PLANE, 0, 0), (HOP, 3, 1),
     (HOP, 2, 3), (PLANE, 1, 0), (HOP, 4, 1), (HOP, 3, 2), (HOP, 2, 4), (HOP, 4, 2),
     (HOP, 3, 3), (PLANE, 2, 0), (HOP, 4, 3), (HOP, 3, 4), (OWNER, 1, 0), (HOP, 4, 4),
     (PLANE, 3, 0), (OWNER, 0, 0), (PLANE, 4, 0), (OWNER, 2, 0), (OWNER, 3, 0), (OWNER, 4, 0),
 )
-LABELS_AT = 10
+LABELS_AT = (6, 7, 11, 12, 16, 19)
 MESH = pl.DeviceIdType.MESH
 
 
@@ -140,11 +140,6 @@
             )
 
     def choose_line():
-        for copy in line_labels:
-            copy.wait_recv()
-        fetch = pltpu.make_async_copy(line_label, line_code, code_sem.at[0])
-        fetch.start()
-        fetch.wait()
         keys = [[jnp.int32(0)] * MINE for _ in range(N_Y)]
         counts = [jnp.int32(0)] * N_Y
         for t in range(N_Z * MINE):
@@ -183,9 +178,6 @@
             )
 
     def choose_plane():
-        fetch = pltpu.make_async_copy(plane_label, plane_code, code_sem.at[1])
-        fetch.start()
-        fetch.wait()
         keys = [jnp.int32(0)] * N_MIC
         for s in range(N_Y * MINE):
             code = plane_code[s // MINE, 0, s % MINE]
@@ -217,20 +209,9 @@
                 m_send.at[c, d - 1], m_recv.at[c, d - 1], at_mic(d),
             )
 
-    line_label[0] = lanes_of([code_of(bin_ref, bin_place_ref, group_ref, j) for j in range(MINE)])
-    line_labels = [
-        send(line_label.at[0], line_label.at[N_Z - d], zl_send.at[d - 1], zl_recv.at[d - 1], at_z(d))
-        for d in range(1, N_Z)
-    ]
     def place_of(s):
         return ((mine_code[s, 0, 0] - 1) >> 6) & (OWN - 1)
-
-    def tables(mine_labels):
-        for copy in mine_labels:
-            copy.wait_recv()
-        fetch = pltpu.make_async_copy(mine_label, mine_code, code_sem.at[2])
-        fetch.start()
-        fetch.wait()
+    def tables():
         slot = lax.broadcasted_iota(jnp.int32, (N_MIC, SIDE), 0)
         focus = jnp.zeros((N_MIC, SIDE), jnp.float32)
         damp = jnp.zeros((N_MIC, SIDE), jnp.float32)
@@ -252,7 +233,6 @@
                 row_sine[:, s : s + 1] * col_sine[s : s + 1, :]
                 + row_cosine[:, s : s + 1] * col_cosine[s : s + 1, :]
             )
-
     def collect(start, depth, source, with_data):
         @pl.loop(0, N_MIC)
         def _(s):
@@ -268,7 +248,6 @@
                     parts[2] = parts[2] + values * values
             for n in range(3 if with_data else 2):
                 sums[s, n] += parts[n][:8] + parts[n][8:]
-
     def correlate():
         slot = lax.broadcasted_iota(jnp.int32, (N_MIC, 128), 0)
         means = []
@@ -282,8 +261,7 @@
         weight = weight.astype(jnp.bfloat16).astype(jnp.float32)
         weights = [jnp.where(mine_code[s, 0, 0] > 0, weight[s, 0], 0.0) for s in range(N_MIC)]
         return correlation, weights
-
-    def update(weights, source, low, high):
+    def chains():
         places = [place_of(s) for s in range(N_MIC)]
         before = []
         for s in range(N_MIC):
@@ -297,7 +275,9 @@
             for s in range(N_MIC):
                 index = jnp.where(places[s] == p, s, index)
             last.append(index)
-
+        return before, last
+
+    def update(weights, source, low, high):
         @pl.loop(low, high)
         def _(i):
             rows = pl.ds(pl.multiple_of(i * ROWS, ROWS), ROWS)
@@ -311,31 +291,52 @@
                 top = total[0, last[p]] + PRIOR_WEIGHT * source[p, rows, :].astype(jnp.float32)
                 out_ref[p, rows, :] = (top / (total[1, last[p]] + PRIOR_WEIGHT)).astype(jnp.bfloat16)
 
+    def read_codes(labels, label, code, n):
+        for copy in labels:
+            copy.wait_recv()
+        fetch = pltpu.make_async_copy(label.at[:, 0:1], code.at[:, 0:1], code_sem.at[n])
+        fetch.start()
+        return fetch
+
     owners_done = []
     for n, (kind, c, h) in enumerate(ORDER):
-        if n == LABELS_AT:
+        if n == 3:
+            line_label[0] = lanes_of([code_of(bin_ref, bin_place_ref, group_ref, j) for j in range(MINE)])
+            line_labels = [
+                send(line_label.at[0, 0:1], line_label.at[N_Z - d, 0:1], zl_send.at[d - 1], zl_recv.at[d - 1], at_z(d))
+                for d in range(1, N_Z)
+            ]
+        if n == LABELS_AT[0]:
+            fetch = read_codes(line_labels, line_label, line_code, 0)
+        if n == LABELS_AT[1]:
+            fetch.wait()
             choose_line()
             plane_labels = [
-                send(pack_label.at[d - 1], plane_label.at[N_Y - d], yl_send.at[d - 1], yl_recv.at[d - 1], at_y(d))
+                send(pack_label.at[d - 1, 0:1], plane_label.at[N_Y - d, 0:1], yl_send.at[d - 1], yl_recv.at[d - 1], at_y(d))
                 for d in range(1, N_Y)
             ]
+        if n == LABELS_AT[2]:
+            fetch = read_codes(plane_labels, plane_label, plane_code, 1)
+        if n == LABELS_AT[3]:
+            fetch.wait()
+            choose_plane()
+            mine_labels = [
+                send(parcel_label.at[d - 1, 0:1], mine_label.at[N_MIC - d, 0:1], ml_send.at[d - 1], ml_recv.at[d - 1], at_mic(d))
+                for d in range(1, N_MIC)
+            ]
+        if n == LABELS_AT[4]:
+            fetch = read_codes(mine_labels, mine_label, mine_code, 2)
+        if n == LABELS_AT[5]:
+            fetch.wait()
+            tables()
         if kind == HOP:
             hop(c, h)
         elif kind == PLANE:
             to_plane(c)
         else:
-            if not owners_done:
-                for copy in plane_labels:
-                    copy.wait_recv()
-                choose_plane()
-                mine_labels = [
-                    send(parcel_label.at[d - 1], mine_label.at[N_MIC - d], ml_send.at[d - 1], ml_recv.at[d - 1], at_mic(d))
-                    for d in range(1, N_MIC)
-                ]
             to_owner(c)
             owners_done.append(c)
-            if len(owners_done) == CHUNKS - 1:
-                tables(mine_labels)
+    before, last = chains()
     loads[8].wait()
     for c in owners_done:
         for d in range(1, N_MIC):
@@ -344,29 +345,29 @@
 
     _, weights = correlate()
     update(weights, refs_ref, 0, SIDE // ROWS)
+    routed = len(copies)
     for s in range(N_MIC):
         for n in range(2):
             sums[s, n] = jnp.zeros((8, SIDE), jnp.float32)
     collect(0, SIDE, out_ref, False)
     correlation, weights = correlate()
 
-    for s in range(N_MIC):
-        tile = jnp.broadcast_to(correlation[s : s + 1, :], (8, 128))
-        if s == 0:
-            row[0] = tile
-        else:
-            row_scores[s - 1] = tile
+    row_scores[...] = correlation
+    row[0:1, :] = correlation[0:1, :]
     by_mic = [
-        send(row_scores.at[d - 1], row.at[N_MIC - d], am_send.at[d - 1], am_recv.at[d - 1], at_mic(d))
+        send(row_scores.at[d : d + 1], row.at[N_MIC - d : N_MIC - d + 1], am_send.at[d - 1], am_recv.at[d - 1], at_mic(d))
         for d in range(1, N_MIC)
     ]
     update(weights, out_ref, 0, SIDE // ROWS // 2)
+    for copy in copies[:routed]:
+        copy.wait_send()
     for copy in by_mic:
         copy.wait_recv()
-    for d in range(N_MIC):
-        plane_scores[0, pl.ds(d, 1), :] = row[d, 0:1, :]
+    lane = lax.broadcasted_iota(jnp.int32, (8, 128), 1)
+    of_mic = lax.broadcasted_iota(jnp.int32, (8, 128), 0)
+    plane_scores[0:1, :] = jnp.sum(jnp.where(lane == of_mic, row[...], 0.0), axis=0, keepdims=True)
     by_y = [
-        send(plane_scores.at[0], plane_scores.at[N_Y - d], ay_send.at[d - 1], ay_recv.at[d - 1], at_y(d))
+        send(plane_scores.at[0:1], plane_scores.at[N_Y - d : N_Y - d + 1], ay_send.at[d - 1], ay_recv.at[d - 1], at_y(d))
         for d in range(1, N_Y)
     ]
     update(weights, out_ref, SIDE // ROWS // 2, SIDE // ROWS)
@@ -379,16 +380,16 @@
     ]
     for copy in by_z:
         copy.wait_recv()
-    lane = lax.broadcasted_iota(jnp.int32, (8, 128), 1)
     scores = jnp.zeros((8, 128), jnp.float32)
     for j in range(MINE):
         owner = bin_place_ref[bin_ref[j]] >> 3
         away_z = ((owner >> 2) - z) & (N_Z - 1)
         away_y = (owner - y) & (N_Y - 1)
         away_mic = ((owner >> 5) - mic) & (N_MIC - 1)
-        scores = jnp.where(lane == j, line_scores[away_z, away_y, pl.ds(away_mic, 1), :], scores)
+        found = jnp.where(lane[0:1, :] == away_mic, line_scores[away_z, pl.ds(away_y, 1), :], 0.0)
+        scores = jnp.where(lane == j, jnp.sum(found, keepdims=True), scores)
     score_ref[...] = scores
-    for copy in copies:
+    for copy in copies[routed:]:
         copy.wait_send()
 
 
@@ -406,7 +407,7 @@
                                      (N_MIC - 1,), (N_Y - 1,), (N_Z - 1,)) for _ in range(2)]
     f32 = [pltpu.VMEM(shape, jnp.float32) for shape in (
         (N_MIC, SIDE, SIDE), (N_MIC, 3, 8, SIDE), (2, N_MIC + 1, ROWS, SIDE),
-        (N_MIC - 1, 8, 128), (N_MIC, 8, 128), (N_Y, 8, 128), (N_Z, N_Y, 8, 128))]
+        (N_MIC, 128), (N_MIC, 128), (N_Y, 128), (N_Z, N_Y, 128))]
     refined, scores = pl.pallas_call(
         kernel,
         out_shape=(

time: 82 us -> 79.3 us (0.967)
  Pallas kernels: 79.3 us -> 76.8 us
    pallas_call x1, Pallas kernels: 79.3 us -> 76.8 us  [body(): pl.pallas_call(kernel, out_shape=(jax.ShapeDtypeStruct((OWN, SIDE, SIDE),...]
where the time goes in v6:
time: 79.3 us; the launch traced here: 79 us
  Pallas kernels  76.8 us (97%)
  local copies, waits for them, and re-layouts  1.48 us (2%)
    pallas_call x1, Pallas kernels, body(): pl.pallas_call(kernel, out_shape=(jax.ShapeDtypeStruct((OWN, SIDE, SIDE),...  76.8 us

profile of v6, /device:TPU:1, one launch (start us, length us, event | category | flops | bytes accessed | tf_op | source)
XLA Modules:
  0.0 79.0 jit_solution(14064155312179735721)
XLA Ops:
  0.6 76.8 %project.1 = (bf16[8,256,256]{2,1,0:T(8,128)(2,1)S(1)}, f32[8,128]{1,0:T(8,128)S(1)}) custom-call(s32[4]{0:T(128)} %refs_0_.1, s32[2048]{0:T(1024)} %refs_1_.1, s32[4]{0:T(128)} %refs_2_.1, s32[2,4]{1,0:T(2,128)} %refs_3_.1, f32[64]{0:T(128)} %refs_4_.1, f32[64]{0:T(128)} %refs_5_.1, bf16[256,256]{1,0:T(8,128)(2,1)} %constant.2.clone.refs_6_, ...), custom_call_target="tpu_custom_call" | custom-call | tf_op jit(solution)/shard_map/project/pallas_call | solution.py:411
  77.5 0.5 slice_bitcast_fusion
  78.0 1.0 %copy.12 = bf16[8,256,256]{2,1,0:T(8,128)(2,1)} copy(bf16[8,256,256]{2,1,0:T(8,128)(2,1)S(1)} %get-tuple-element.8) | data formatting | bytes 2097152

commit v7 on v6

--- a/solution.py
+++ b/solution.py
@@ -256,11 +256,12 @@
             for s in range(N_MIC):
                 mean = jnp.where(slot == s, jnp.sum(sums[s, n], keepdims=True), mean)
             means.append(mean / PIXELS)
-        correlation = means[0] / jnp.sqrt((means[1] + EPSILON) * (means[2] + EPSILON))
+        return means[0] / jnp.sqrt((means[1] + EPSILON) * (means[2] + EPSILON))
+
+    def weigh(correlation):
         weight = 1.0 / (1.0 + jnp.exp(-SIDE * correlation))
         weight = weight.astype(jnp.bfloat16).astype(jnp.float32)
-        weights = [jnp.where(mine_code[s, 0, 0] > 0, weight[s, 0], 0.0) for s in range(N_MIC)]
-        return correlation, weights
+        return [jnp.where(mine_code[s, 0, 0] > 0, weight[s, 0], 0.0) for s in range(N_MIC)]
     def chains():
         places = [place_of(s) for s in range(N_MIC)]
         before = []
@@ -343,14 +344,13 @@
             m_copies[c, d].wait_recv()
         collect(STARTS[c], DEPTHS[c], refs_ref, True)
 
-    _, weights = correlate()
-    update(weights, refs_ref, 0, SIDE // ROWS)
+    update(weigh(correlate()), refs_ref, 0, SIDE // ROWS)
     routed = len(copies)
     for s in range(N_MIC):
         for n in range(2):
             sums[s, n] = jnp.zeros((8, SIDE), jnp.float32)
     collect(0, SIDE, out_ref, False)
-    correlation, weights = correlate()
+    correlation = correlate()
 
     row_scores[...] = correlation
     row[0:1, :] = correlation[0:1, :]
@@ -358,6 +358,7 @@
         send(row_scores.at[d : d + 1], row.at[N_MIC - d : N_MIC - d + 1], am_send.at[d - 1], am_recv.at[d - 1], at_mic(d))
         for d in range(1, N_MIC)
     ]
+    weights = weigh(correlation)
     update(weights, out_ref, 0, SIDE // ROWS // 2)
     for copy in copies[:routed]:
         copy.wait_send()

time: 79.3 us -> 79.2 us (level)
  no operation moved by 1% of the time
where the time goes in v7:
time: 79.2 us; the launch traced here: 78.9 us
  Pallas kernels  76.8 us (97%)
  local copies, waits for them, and re-layouts  1.48 us (2%)
    pallas_call x1, Pallas kernels, body(): pl.pallas_call(kernel, out_shape=(jax.ShapeDtypeStruct((OWN, SIDE, SIDE),...  76.8 us

profile of v7, /device:TPU:1, one launch (start us, length us, event | category | flops | bytes accessed | tf_op | source)
XLA Modules:
  0.0 78.9 jit_solution(13249014728039684162)
XLA Ops:
  0.6 76.8 %project.1 = (bf16[8,256,256]{2,1,0:T(8,128)(2,1)S(1)}, f32[8,128]{1,0:T(8,128)S(1)}) custom-call(s32[4]{0:T(128)} %refs_0_.1, s32[2048]{0:T(1024)} %refs_1_.1, s32[4]{0:T(128)} %refs_2_.1, s32[2,4]{1,0:T(2,128)} %refs_3_.1, f32[64]{0:T(128)} %refs_4_.1, f32[64]{0:T(128)} %refs_5_.1, bf16[256,256]{1,0:T(8,128)(2,1)} %constant.2.clone.refs_6_, ...), custom_call_target="tpu_custom_call" | custom-call | tf_op jit(solution)/shard_map/project/pallas_call | solution.py:412
  77.5 0.5 slice_bitcast_fusion
  78.0 1.0 %copy.12 = bf16[8,256,256]{2,1,0:T(8,128)(2,1)} copy(bf16[8,256,256]{2,1,0:T(8,128)(2,1)S(1)} %get-tuple-element.8) | data formatting | bytes 2097152
